TPU v7x, 128 devices: a whole 4x4x4 slice. The times are simulated.
128 devices in a mesh: dp: 16 (over z, y), expert: 8 (over x, core).
Axes of the slice: x: 4, y: 4, z: 4, core: 2. Of those that a mesh axis runs over, the one named last changes fastest.
Arguments:
- records: bfloat16 [32, 128, 8192], P('dp', None, 'expert'), may hold values from -110 to 110
- pair_blocks: int32 [16, 2], replicated, may hold values from 0 to 31
- lengths: int32 [16], replicated, may hold values from 64 to 256
- norm_gain: float32 [6144], replicated, may hold values from 0.25 to 1.75
- gate_logits: float32 [4096, 2], P('dp'), may hold values from -6 to 6
- expert_ids: int32 [4096, 2], P('dp'), may hold values from 0 to 7, all different within a row; in each aligned block of 256 rows (0 to 255, 256 to 511, ...) at most 80 rows name the same one
- gate_weight: bfloat16 [8, 6144, 8192], P('expert', None, 'dp'), may hold values from -0.078125 to 0.078125
- up_weight: bfloat16 [8, 6144, 8192], P('expert', None, 'dp'), may hold values from -0.078125 to 0.078125
- down_weight: bfloat16 [8, 8192, 6144], P('expert', 'dp'), may hold values from -0.0625 to 0.0625
Outputs:
- layer_out: bfloat16 [4096, 6144], P('dp', 'expert')
Inputs may be any that keep to these rules, and one draw needn't show every extreme that they name: `expert_ids`: A token's 2 experts differ. Among the tokens of one prompt no expert is chosen more than 80 times.
All inputs are finite; a program needn't handle non-finite values.
Results may differ from a plain program's by a relative error of at most 0.018.
Values may be sent and summed in bfloat16 or wider, within the bound.
No kernel may reach another device: no remote copies, remote signals or barrier semaphores. Data moves between devices by JAX's collectives and lax.ppermute only.
A program may use at most 128 MiB of HBM per device.

v0:
```python
import math

import jax
import jax.numpy as jnp
from jax import lax
from jax.sharding import PartitionSpec as P

HEAD_SIZE = 128
TOP = 2
BLOCK_TOKENS = 128
PROMPT_TOKENS = 256
QUERY_GROUP = 6


def route_table(expert_block, expert_count, capacity):
    flattened = expert_block.reshape(-1)
    total = flattened.shape[0]
    one_hot = (flattened[:, None] == jnp.arange(expert_count, dtype=jnp.int32)[None, :]).astype(
        jnp.int32
    )
    earlier = jnp.cumsum(one_hot, axis=0) - one_hot
    slot_index = jnp.sum(earlier * one_hot, axis=1)
    token_index = jnp.arange(total, dtype=jnp.int32) // expert_block.shape[1]
    table = (
        jnp.full((expert_count, capacity), -1, jnp.int32).at[flattened, slot_index].set(token_index)
    )
    return (table, flattened * capacity + slot_index)


def body(
    records,
    pair_blocks,
    lengths,
    norm_gain,
    gate_logits,
    expert_ids,
    gate_weight,
    up_weight,
    down_weight,
):
    dp_index = lax.axis_index("dp")
    block_count = PROMPT_TOKENS // BLOCK_TOKENS
    wanted = lax.dynamic_index_in_dim(pair_blocks, dp_index, 0, keepdims=False)
    key_limit = lax.dynamic_index_in_dim(lengths, dp_index, 0, keepdims=False)
    col_width = records.shape[2]
    blank_rows = jnp.zeros((block_count, BLOCK_TOKENS, col_width), jnp.bfloat16)
    shard_rows = lax.all_gather(records, "dp", axis=0, tiled=True)
    row_count = shard_rows.shape[0]
    is_wanted = wanted[:, None] == jnp.arange(row_count, dtype=jnp.int32)[None, :]
    chosen = jnp.einsum(
        "jn,nrc->jrc",
        is_wanted.astype(jnp.bfloat16),
        shard_rows,
        preferred_element_type=jnp.float32,
    )
    prompt_rows = jnp.where(
        jnp.any(is_wanted, axis=1)[:, None, None], chosen.astype(jnp.bfloat16), blank_rows
    )
    local_heads = col_width // ((QUERY_GROUP + 2) * HEAD_SIZE)
    rows_of_tokens = prompt_rows.reshape(PROMPT_TOKENS, local_heads, QUERY_GROUP + 2, HEAD_SIZE)
    queries = rows_of_tokens[:, :, :QUERY_GROUP, :]
    key_vecs = rows_of_tokens[:, :, QUERY_GROUP, :]
    value_vecs = rows_of_tokens[:, :, QUERY_GROUP + 1, :]
    scores = jnp.einsum("rhgd,khd->hgrk", queries, key_vecs, preferred_element_type=jnp.float32) * (
        1.0 / math.sqrt(HEAD_SIZE)
    )
    positions = jnp.arange(PROMPT_TOKENS, dtype=jnp.int32)
    allowed = (positions[None, :] <= positions[:, None]) & (positions[None, :] < key_limit)
    scores = jnp.where(allowed, scores, -jnp.inf)
    row_max = jnp.max(scores, axis=-1, keepdims=True)
    exponent = jnp.exp(scores - row_max)
    weights_bf = (exponent / jnp.sum(exponent, axis=-1, keepdims=True)).astype(jnp.bfloat16)
    mixed = jnp.einsum("hgrk,khd->rhgd", weights_bf, value_vecs, preferred_element_type=jnp.float32)
    attended = mixed.astype(jnp.bfloat16).reshape(
        PROMPT_TOKENS, local_heads * QUERY_GROUP * HEAD_SIZE
    )
    local_width = attended.shape[1]
    expert_count = lax.axis_size("expert")
    capacity = 5 * PROMPT_TOKENS * TOP // (4 * expert_count)
    table, flat_rows = route_table(expert_ids, expert_count, capacity)
    outgoing = jnp.where(
        (table >= 0)[:, :, None], attended[jnp.maximum(table, 0)], jnp.zeros((), jnp.bfloat16)
    )
    arrived = lax.all_to_all(outgoing, "expert", split_axis=0, concat_axis=2, tiled=True)[0]
    arrived_f = arrived.astype(jnp.float32)
    mean_square = jnp.mean(arrived_f * arrived_f, axis=1, keepdims=True)
    normed = (arrived_f * lax.rsqrt(mean_square + 1e-05) * norm_gain).astype(jnp.bfloat16)
    gate_local = gate_weight[0]
    up_local = up_weight[0]
    down_local = down_weight[0]
    slot_rows = lax.all_gather(normed, "dp", axis=0, tiled=True)
    gate_part = jnp.dot(slot_rows, gate_local, preferred_element_type=jnp.float32)
    up_part = jnp.dot(slot_rows, up_local, preferred_element_type=jnp.float32)
    hidden = (jax.nn.silu(gate_part) * up_part).astype(jnp.bfloat16)
    totals = lax.psum(
        jnp.dot(hidden, down_local, preferred_element_type=jnp.float32).astype(jnp.bfloat16), "dp"
    ).astype(jnp.float32)
    summed = lax.dynamic_slice_in_dim(totals, dp_index * capacity, capacity, 0)
    expert_out = summed.astype(jnp.bfloat16)
    returned = lax.all_to_all(expert_out[None], "expert", split_axis=2, concat_axis=0, tiled=True)
    picked = returned.reshape(expert_count * capacity, local_width)[flat_rows].reshape(
        PROMPT_TOKENS, TOP, local_width
    )
    gate_weights = jax.nn.softmax(gate_logits, axis=-1)
    combined = attended.astype(jnp.float32) + jnp.sum(
        gate_weights[:, :, None] * picked.astype(jnp.float32), axis=1
    )
    return combined.astype(jnp.bfloat16)


def solution(mesh):
    placed = (
        P("dp", None, "expert"),
        P(),
        P(),
        P(),
        P("dp", None),
        P("dp", None),
        P("expert", None, "dp"),
        P("expert", None, "dp"),
        P("expert", "dp", None),
    )
    return jax.shard_map(
        body, mesh=mesh, in_specs=placed, out_specs=P("dp", "expert"), check_vma=False
    )
```

profile of v0, /device:TPU:1, one launch (start us, length us, event | category | flops | bytes accessed | tf_op | source)
XLA Modules:
  0.0 568.1 jit_solution(10639398049815429231)
XLA Ops:
  8.8 1.2 dynamic_slice.12
  10.0 1.1 reduce-window.6
  11.5 22.1 %scatter_fusion = s32[8,80]{1,0:T(8,128)S(1)} fusion(s32[8,80]{1,0:T(8,128)S(1)} %broadcast_in_dim.62, s32[512]{0:T(512)S(1)} %bitcast.92, s32[512]{0:T(512)S(1)} %add_select_fusion), kind=kCustom, calls=%fused_computation.2 | custom fusion | bytes 10240 | tf_op jit(solution)/shard_map/scatter | solution.py:25
  34.7 49.0 %all-gather.3.cloned.1.call-done = bf16[32,128,1024]{2,1,0:T(8,128)(2,1)} async-done(((bf16[2,128,1024]{2,1,0:T(8,128)(2,1)}), bf16[32,128,1024]{2,1,0:T(8,128)(2,1)}) %all-gather.3.cloned.1.call-update) | async-done | bytes 8388624 | tf_op jit(solution)/shard_map/all_gather | solution.py:47
  83.6 12.5 %broadcast_select_fusion = bf16[2,128,1024]{2,0,1:T(2,128)(2,1)S(1)} fusion(pred[2]{0:T(512)(128)(4,1)S(1)} %fusion.34, bf16[32,128,1024]{2,1,0:T(8,128)(2,1)} %all-gather.3.cloned.1.call-done, s32[2]{0:T(128)S(1)} %dynamic-slice_reduce_fusion), kind=kOutput, calls=%fused_computation.25 | convolution fusion | flops 17301568 | bytes 8912906 | tf_op jit(solution)/shard_map/jn,nrc->jrc/dot_general | solution.py:50
  98.0 3.4 gather_fusion
  101.6 19.2 %all_to_all.24 = bf16[8,80,768]{2,1,0:T(8,128)(2,1)S(1)} all-to-all(bf16[8,80,768]{2,1,0:T(8,128)(2,1)S(1)} %broadcast_select_fusion.1), channel_id=1, replica_groups=mesh['dp'=16,'expert'=8] {'expert'}, dimensions={0} | all-to-all | bytes 1966080 | tf_op jit(solution)/shard_map/all_to_all | solution.py:84
  121.6 1.2 multiply_convert_fusion
  122.9 104.2 %all-gather.5.cloned.1.call-done = bf16[1280,6144]{1,0:T(8,128)(2,1)} async-done(((bf16[80,6144]{1,0:T(8,128)(2,1)}), bf16[1280,6144]{1,0:T(8,128)(2,1)}) %all-gather.5.cloned.1.call-update) | async-done | bytes 15728656 | tf_op jit(solution)/shard_map/all_gather | solution.py:91
  227.1 14.7 %fusion.5 = f32[1280,512]{1,0:T(8,128)} fusion(bf16[1280,6144]{1,0:T(8,128)(2,1)} %all-gather.5.cloned.1.call-done, bf16[1,6144,512]{2,1,0:T(8,128)(2,1)} %param.15), kind=kOutput, calls=%fused_computation.9 | convolution fusion | flops 8053063680 | bytes 24641536 | tf_op jit(solution)/shard_map/dot_general | solution.py:92
  241.8 11.7 %fusion.10 = bf16[1280,512]{1,0:T(8,128)(2,1)S(1)} fusion(bf16[1280,6144]{1,0:T(8,128)(2,1)S(1)} %copy-done.5, bf16[1,6144,512]{2,1,0:T(8,128)(2,1)} %param.16, f32[1280,512]{1,0:T(8,128)} %fusion.5), kind=kOutput, calls=%fused_computation.12 | convolution fusion | flops 8056995840 | bytes 25952256 | tf_op jit(solution)/shard_map/dot_general | solution.py:93
  253.5 11.1 %convolution_convert_fusion = bf16[1280,6144]{1,0:T(8,128)(2,1)} fusion(bf16[1280,512]{1,0:T(8,128)(2,1)S(1)} %fusion.10, bf16[1,512,6144]{2,1,0:T(8,128)(2,1)S(1)} %bitcast.106), kind=kOutput, calls=%fused_computation.3 | convolution fusion | flops 8060928000 | bytes 23330816 | tf_op jit(solution)/shard_map/dot_general | solution.py:96
  264.6 209.7 %all-reduce.2.cloned.1.call-done = bf16[1280,6144]{1,0:T(8,128)(2,1)} async-done(((bf16[1280,6144]{1,0:T(8,128)(2,1)}), bf16[1280,6144]{1,0:T(8,128)(2,1)}) %all-reduce.2.cloned.1.call-update) | async-done | bytes 15728656 | tf_op jit(solution)/shard_map/psum | solution.py:95
  474.4 2.2 fusion.18
  476.6 6.7 %copy.60 = bf16[1,80,6144]{1,0,2:T(2,128)(2,1)S(1)} copy(bf16[1,80,6144]{2,1,0:T(8,128)(2,1)} %fusion.18) | data formatting | bytes 1966080 | tf_op jit(solution)/shard_map/broadcast_in_dim | solution.py:100
  483.8 34.6 %reduce.9 = bf16[6144,80]{1,0:T(8,128)(2,1)} reduce(bf16[6144,1,80]{2,1,0:T(2,128)(2,1)S(1)} %bitcast.93, bf16[]{:T(256)} %broadcast.159), dimensions={1}, to_apply=%bitcast.77.reduce_sub_computation | reduce | bytes 1966082
  518.5 5.4 reshape.198
  523.8 5.2 all-to-all-start.1
  529.9 13.6 %all-to-all-done.1 = bf16[8,2,30720]{2,1,0:T(2,128)(2,1)} async-done(((bf16[8,2,30720]{2,1,0:T(2,128)(2,1)}), bf16[8,2,30720]{2,1,0:T(2,128)(2,1)}, u32[]{:S(2)}, u32[]{:S(2)}) %all-to-all-start.1) | async-done | bytes 983072 | tf_op jit(solution)/shard_map/all_to_all | solution.py:100
  543.5 5.6 reshape.199
  549.1 5.1 copy.61
  554.1 1.4 copy.69
  555.8 2.0 gather_fusion.1
  558.6 1.9 multiply_reduce_fusion
  (66 shorter events, 9.7 us)
Async XLA Ops:
  6.5 2.0 copy-start
  6.5 77.1 %all-gather.3.cloned.1.call-start = ((), (), s32[]{:S(2)}) async-start(), calls=%async_computation.2 | async-start | bytes 8912896 | tf_op jit(solution)/shard_map/all_gather | solution.py:47
  7.3 219.8 %all-gather.5.cloned.1.call-start = ((), (), s32[]{:S(2)}) async-start(), calls=%async_computation.3 | async-start | bytes 16711680 | tf_op jit(solution)/shard_map/all_gather | solution.py:91
  120.9 0.7 copy-start.3
  122.9 351.5 %all-reduce.2.cloned.1.call-start = ((), (), s32[]{:S(2)}) async-start(), calls=%async_computation.4 | async-start | bytes 31457280 | tf_op jit(solution)/shard_map/psum | solution.py:95
  227.1 14.7 %copy-start.5 = (bf16[1280,6144]{1,0:T(8,128)(2,1)S(1)}, bf16[1280,6144]{1,0:T(8,128)(2,1)}, u32[]{:S(2)}) copy-start(bf16[1280,6144]{1,0:T(8,128)(2,1)} %all-gather.5.cloned.1.call-done) | copy-start | bytes 47185924
  227.1 26.4 %slice-start = ((s8[6291456]{0:T(1024)(128)(4,1)}), s8[4194304]{0:T(1024)(128)(4,1)S(1)}, s32[]{:S(2)}) async-start(s8[6291456]{0:T(1024)(128)(4,1)} %bitcast.105), calls=%async_computation.5 | async-start | bytes 8388608
  241.8 11.7 %slice-start.1 = ((s8[6291456]{0:T(1024)(128)(4,1)}), s8[2097152]{0:T(1024)(128)(4,1)S(1)}, s32[]{:S(2)}) async-start(s8[6291456]{0:T(1024)(128)(4,1)} %bitcast.105), calls=%async_computation.6 | async-start | bytes 4194304
  518.5 10.6 %copy-start.4 = (f32[256,2]{0,1:T(2,128)S(1)}, f32[256,2]{0,1:T(2,128)}, u32[]{:S(2)}) copy-start(f32[256,2]{0,1:T(2,128)} %param.13) | copy-start | bytes 6148
  523.8 19.6 %all-to-all-start.1 = ((bf16[8,2,30720]{2,1,0:T(2,128)(2,1)}), bf16[8,2,30720]{2,1,0:T(2,128)(2,1)}, u32[]{:S(2)}, u32[]{:S(2)}) async-start(bf16[8,2,30720]{2,1,0:T(2,128)(2,1)} %reshape.198), calls=%async_computation.1 | async-start | bytes 1966080 | tf_op jit(solution)/shard_map/all_to_all | solution.py:100
  555.8 2.8 copy-start.2
  557.8 3.5 copy-start.1
Sparse Core Ops, SparseCore 0:
  9.5 74.0 all-gather.2
  123.0 104.0 all-gather.4
  264.8 209.5 all-reduce.1
where the time goes:
time: 578 us; the launch traced here: 568 us
  waiting for transfers between devices  377 us (65%)
  local copies, waits for them, and re-layouts  58.1 us (10%)
  matrix products  50.8 us (9%)
  other arithmetic  43.9 us (8%)
  blocking collectives  19.2 us (3%)
  between operations  13.7 us (2%)
    psum x1, waiting for transfers between devices, body(): lax.psum(jnp.dot(hidden, down_local, preferred_element_type=jnp.float32)....  210 us
    all_gather x1, waiting for transfers between devices, body(): slot_rows = lax.all_gather(normed, 'dp', axis=0, tiled=True)  104 us
    all_gather x1, waiting for transfers between devices, body(): shard_rows = lax.all_gather(records, 'dp', axis=0, tiled=True)  49 us
    unnamed x3, other arithmetic  34.8 us
    scatter x1, local copies, waits for them, and re-layouts, route_table(): jnp.full((expert_count, capacity), -1, jnp.int32).at[flattened, slot_index]  22.1 us
    all_to_all x1, blocking collectives, body(): lax.all_to_all(outgoing, 'expert', split_axis=0, concat_axis=2, tiled=True)  19.2 us
    dot_general x1, matrix products, body(): jnp.dot(slot_rows, gate_local, preferred_element_type=jnp.float32)  14.7 us
    unnamed x24, local copies, waits for them, and re-layouts  14.3 us
  transfers between devices with their start and end apart: 4, of which 4 were waited for; matrix products, arithmetic and copies ran while one was open for 5% of the time, Pallas kernels for 0%

commit v1 on v0

v1 whole, which is shorter than its diff:
```python
import math

import jax
import jax.numpy as jnp
from jax import lax
from jax.experimental import pallas as pl
from jax.experimental.pallas import tpu as pltpu
from jax.sharding import Mesh
from jax.sharding import PartitionSpec as P

HEAD = 128
GROUP = 6
BLOCK = 128
PROMPT = 256
EXPERTS = 8
CAP = 80
WIDTH = 768
D = 6144
FF_DEV = 512
N_DP = 16
SIDE = 4
QKV = 1024


def pick_kernel(idx_ref, mine_ref, blocks_ref, out_ref):
    i = pl.program_id(0)

    @pl.when(mine_ref[i] == 1)
    def _():
        out_ref[...] = blocks_ref[...]

    @pl.when(mine_ref[i] == 0)
    def _():
        out_ref[...] = jnp.zeros_like(out_ref)


def pick_blocks(idx, mine, blocks):
    n, (_, rows, cols) = idx.shape[0], blocks.shape
    return pl.pallas_call(
        pick_kernel,
        grid_spec=pltpu.PrefetchScalarGridSpec(
            num_scalar_prefetch=2,
            grid=(n,),
            in_specs=[pl.BlockSpec((1, rows, cols), lambda i, idx, mine: (idx[i], 0, 0))],
            out_specs=pl.BlockSpec((1, rows, cols), lambda i, idx, mine: (i, 0, 0)),
        ),
        out_shape=jax.ShapeDtypeStruct((n, rows, cols), blocks.dtype),
        name="pick_blocks",
    )(idx, mine, blocks)


def attend_kernel(len_ref, rows_ref, ids_ref, att_ref, out_ref):
    limit = len_ref[0]
    scale = 1.0 / math.sqrt(HEAD)
    for top in (0, BLOCK):
        span = top + BLOCK
        keys = rows_ref[0:span, GROUP * HEAD : (GROUP + 1) * HEAD]
        values = rows_ref[0:span, (GROUP + 1) * HEAD : (GROUP + 2) * HEAD]
        row = lax.broadcasted_iota(jnp.int32, (BLOCK, span), 0) + top
        col = lax.broadcasted_iota(jnp.int32, (BLOCK, span), 1)
        allowed = (col <= row) & (col < limit)
        for g in range(GROUP):
            query = rows_ref[top:span, g * HEAD : (g + 1) * HEAD]
            scores = lax.dot_general(
                query, keys, (((1,), (1,)), ((), ())), preferred_element_type=jnp.float32
            )
            scores = jnp.where(allowed, scores * scale, -jnp.inf)
            exponent = jnp.exp(scores - jnp.max(scores, axis=1, keepdims=True))
            probs = (exponent / jnp.sum(exponent, axis=1, keepdims=True)).astype(jnp.bfloat16)
            mixed = jnp.dot(probs, values, preferred_element_type=jnp.float32)
            att_ref[top:span, g * HEAD : (g + 1) * HEAD] = mixed.astype(jnp.bfloat16)
    names = lax.broadcasted_iota(jnp.int32, (EXPERTS, PROMPT), 0)
    named = (ids_ref[0:1, :] == names) | (ids_ref[1:2, :] == names)
    first = lax.broadcasted_iota(jnp.int32, (PROMPT, PROMPT), 0)
    second = lax.broadcasted_iota(jnp.int32, (PROMPT, PROMPT), 1)
    before = jnp.where(first < second, 1.0, 0.0).astype(jnp.bfloat16)
    taken = jnp.where(named, 1.0, 0.0)
    slot = jnp.dot(taken.astype(jnp.bfloat16), before, preferred_element_type=jnp.float32)
    slot = jnp.where(named, slot, -1.0).astype(jnp.int32)
    att = att_ref[...]
    place = lax.broadcasted_iota(jnp.int32, (CAP, PROMPT), 0)
    for e in range(EXPERTS):
        chosen = jnp.where(place == slot[e : e + 1, :], 1.0, 0.0).astype(jnp.bfloat16)
        sent = jnp.dot(chosen, att, preferred_element_type=jnp.float32)
        out_ref[e * CAP : (e + 1) * CAP, :] = sent.astype(jnp.bfloat16)


def attend(limit, rows, ids_t):
    return pl.pallas_call(
        attend_kernel,
        in_specs=[
            pl.BlockSpec(memory_space=pltpu.SMEM),
            pl.BlockSpec(memory_space=pltpu.VMEM),
            pl.BlockSpec(memory_space=pltpu.VMEM),
        ],
        out_specs=[pl.BlockSpec(memory_space=pltpu.VMEM), pl.BlockSpec(memory_space=pltpu.VMEM)],
        out_shape=[
            jax.ShapeDtypeStruct((PROMPT, WIDTH), jnp.bfloat16),
            jax.ShapeDtypeStruct((EXPERTS * CAP, WIDTH), jnp.bfloat16),
        ],
        compiler_params=pltpu.CompilerParams(vmem_limit_bytes=32 << 20),
        name="attend",
    )(limit, rows, ids_t)


def norm_kernel(x_ref, gain_ref, out_ref):
    total = jnp.zeros((CAP, 1), jnp.float32)
    for i in range(EXPERTS):
        part = x_ref[i].astype(jnp.float32)
        total = total + jnp.sum(part * part, axis=1, keepdims=True)
    factor = lax.rsqrt(total * (1.0 / D) + 1e-05)
    for i in range(EXPERTS):
        cols = slice(i * WIDTH, (i + 1) * WIDTH)
        out_ref[:, cols] = (x_ref[i].astype(jnp.float32) * factor * gain_ref[:, cols]).astype(
            jnp.bfloat16
        )


def normalise(arrived, gain):
    return pl.pallas_call(
        norm_kernel,
        out_shape=jax.ShapeDtypeStruct((CAP, D), jnp.bfloat16),
        compiler_params=pltpu.CompilerParams(vmem_limit_bytes=32 << 20),
        name="normalise",
    )(arrived, gain)


def ffn_kernel(x_ref, gate_ref, up_ref, down_ref, out_ref):
    x = x_ref[...]
    gate = jnp.dot(x, gate_ref[0], preferred_element_type=jnp.float32)
    up = jnp.dot(x, up_ref[0], preferred_element_type=jnp.float32)
    hidden = (gate / (1.0 + jnp.exp(-gate)) * up).astype(jnp.bfloat16)
    n = x.shape[0] // CAP
    for i in range(EXPERTS):
        part = jnp.dot(
            hidden, down_ref[0, :, i * WIDTH : (i + 1) * WIDTH], preferred_element_type=jnp.float32
        ).astype(jnp.bfloat16)
        for j in range(n):
            out_ref[j, i] = part[j * CAP : (j + 1) * CAP]


def ffn(slot_rows, gate, up, down, tile):
    n = slot_rows.shape[0]
    whole = lambda i: (0, 0, 0)
    return pl.pallas_call(
        ffn_kernel,
        grid=(n // tile,),
        in_specs=[
            pl.BlockSpec((tile, D), lambda i: (i, 0)),
            pl.BlockSpec((1, D, FF_DEV), whole, pipeline_mode=pl.Buffered(1)),
            pl.BlockSpec((1, D, FF_DEV), whole, pipeline_mode=pl.Buffered(1)),
            pl.BlockSpec((1, FF_DEV, D), whole, pipeline_mode=pl.Buffered(1)),
        ],
        out_specs=pl.BlockSpec((tile // CAP, EXPERTS, CAP, WIDTH), lambda i: (i, 0, 0, 0)),
        out_shape=jax.ShapeDtypeStruct((n // CAP, EXPERTS, CAP, WIDTH), jnp.bfloat16),
        compiler_params=pltpu.CompilerParams(vmem_limit_bytes=56 << 20),
        name="ffn",
    )(slot_rows, gate, up, down)


def combine_kernel(att_ref, ret_ref, ids_ref, logits_ref, out_ref):
    names = lax.broadcasted_iota(jnp.int32, (PROMPT, HEAD), 1)
    ids = [ids_ref[:, c : c + 1] for c in range(2)]
    named = (ids[0] == names) | (ids[1] == names)
    first = lax.broadcasted_iota(jnp.int32, (PROMPT, PROMPT), 0)
    second = lax.broadcasted_iota(jnp.int32, (PROMPT, PROMPT), 1)
    before = jnp.where(second < first, 1.0, 0.0).astype(jnp.bfloat16)
    taken = jnp.where(named, 1.0, 0.0).astype(jnp.bfloat16)
    count = jnp.dot(before, taken, preferred_element_type=jnp.float32)
    logits = [logits_ref[:, c : c + 1] for c in range(2)]
    top = jnp.maximum(logits[0], logits[1])
    exps = [jnp.exp(v - top) for v in logits]
    total = exps[0] + exps[1]
    ret = ret_ref[...]
    column = lax.broadcasted_iota(jnp.int32, (PROMPT, EXPERTS * CAP), 1)
    mixed = None
    for c in range(2):
        slot = jnp.sum(jnp.where(ids[c] == names, count, 0.0), axis=1, keepdims=True)
        at = ids[c] * CAP + slot.astype(jnp.int32)
        chosen = jnp.where(column == at, 1.0, 0.0).astype(jnp.bfloat16)
        picked = jnp.dot(chosen, ret, preferred_element_type=jnp.float32)
        term = exps[c] / total * picked
        mixed = term if mixed is None else mixed + term
    out_ref[...] = (att_ref[...].astype(jnp.float32) + mixed).astype(jnp.bfloat16)


def combine(att, returned, ids, logits):
    return pl.pallas_call(
        combine_kernel,
        out_shape=jax.ShapeDtypeStruct((PROMPT, WIDTH), jnp.bfloat16),
        compiler_params=pltpu.CompilerParams(vmem_limit_bytes=32 << 20),
        name="combine",
    )(att, returned, ids, logits)


def fetch_rows(records, pair_blocks):
    z, y = lax.axis_index("z"), lax.axis_index("y")
    column = lax.all_gather(records, "z", axis=0, tiled=True)
    wanted = lax.dynamic_slice_in_dim(pair_blocks, z * SIDE, SIDE, 0).reshape(-1)
    owner = wanted // 2
    mine = (owner % SIDE == y).astype(jnp.int32)
    idx = (owner // SIDE) * 2 + wanted % 2
    picked = pick_blocks(idx, mine, column)
    return lax.psum_scatter(picked, "y", scatter_dimension=0, tiled=True)


def body(
    records,
    pair_blocks,
    lengths,
    norm_gain,
    gate_logits,
    expert_ids,
    gate_weight,
    up_weight,
    down_weight,
):
    dp_index = lax.axis_index("z") * SIDE + lax.axis_index("y")
    limit = lax.dynamic_slice_in_dim(lengths, dp_index, 1, 0)
    rows = fetch_rows(records, pair_blocks).reshape(PROMPT, QKV)
    att, outgoing = attend(limit, rows, expert_ids.T)
    arrived = lax.all_to_all(
        outgoing.reshape(EXPERTS, CAP, WIDTH), "expert", split_axis=0, concat_axis=0, tiled=True
    )
    normed = normalise(arrived, norm_gain.reshape(1, D))
    slot_rows = lax.all_gather(normed, ("z", "y"), axis=0, tiled=True)
    partial = ffn(slot_rows, gate_weight, up_weight, down_weight, 320)
    summed = lax.psum_scatter(partial, ("z", "y"), scatter_dimension=0, tiled=True)
    returned = lax.all_to_all(summed[0], "expert", split_axis=0, concat_axis=0, tiled=True)
    return combine(att, returned.reshape(EXPERTS * CAP, WIDTH), expert_ids, gate_logits)


def solution(mesh):
    fine = Mesh(mesh.devices.reshape(SIDE, SIDE, EXPERTS), ("z", "y", "expert"))
    dp = ("z", "y")
    placed = (
        P(dp, None, "expert"),
        P(),
        P(),
        P(),
        P(dp, None),
        P(dp, None),
        P("expert", None, dp),
        P("expert", None, dp),
        P("expert", dp, None),
    )
    return jax.shard_map(
        body, mesh=fine, in_specs=placed, out_specs=P(dp, "expert"), check_vma=False
    )
```

time: 578 us -> 379 us (0.66); the launches traced: 568 us -> 378 us
  waiting for transfers between devices: 377 us -> 288 us
  local copies, waits for them, and re-layouts: 58.1 us -> 2.17 us
  matrix products: 50.8 us -> 0 us
  Pallas kernels: 0 us -> 48.6 us
  other arithmetic: 43.9 us -> 1.13 us
    psum x1 -> x0, waiting for transfers between devices: 210 us -> none  [body(): lax.psum(jnp.dot(hidden, down_local, preferred_element_type=jnp.float32)....]
    unnamed x3 -> x5, waiting for transfers between devices: 0.74 us -> 106 us
    dot_general x6 -> x0, matrix products: 50.8 us -> none  [the longest x1 14.7 us: body(): jnp.dot(slot_rows, gate_local, preferred_element_type=jnp.float32)]
    pallas_call x0 -> x5, Pallas kernels: none -> 48.6 us  [the longest x1 34.9 us: ffn(): pl.pallas_call(ffn_kernel, grid=(n // tile,), in_specs=[pl.BlockSpec((til...]
    unnamed x3 -> x0, other arithmetic: 34.8 us -> none
    reduce_scatter x0 -> x1, waiting for transfers between devices: none -> 29.5 us  [fetch_rows(): return lax.psum_scatter(picked, 'y', scatter_dimension=0, tiled=True)]
    scatter x1 -> x0, local copies, waits for them, and re-layouts: 22.1 us -> none  [route_table(): jnp.full((expert_count, capacity), -1, jnp.int32).at[flattened, slot_index]]
    all_gather x2, waiting for transfers between devices: 153 us -> 139 us  [the longest x1 104 us: body(): slot_rows = lax.all_gather(normed, ('z', 'y'), axis=0, tiled=True)]
  transfers between devices with their start and end apart: 4 -> 5, of which waited for: 4 -> 5; matrix products, arithmetic and copies ran while one was open for 5% -> 1% of each run, Pallas kernels for 0% -> 0%
where the time goes in v1:
time: 379 us; the launch traced here: 378 us
  waiting for transfers between devices  288 us (76%)
  Pallas kernels  48.6 us (13%)
  blocking collectives  19.1 us (5%)
  between operations  13.2 us (3%)
  starting transfers between devices  5.45 us (1%)
    unnamed x5, waiting for transfers between devices  106 us
    all_gather x1, waiting for transfers between devices, body(): slot_rows = lax.all_gather(normed, ('z', 'y'), axis=0, tiled=True)  104 us
    pallas_call x1, Pallas kernels, ffn(): pl.pallas_call(ffn_kernel, grid=(n // tile,), in_specs=[pl.BlockSpec((til...  34.9 us
    all_gather x1, waiting for transfers between devices, fetch_rows(): column = lax.all_gather(records, 'z', axis=0, tiled=True)  34.6 us
    reduce_scatter x1, waiting for transfers between devices, fetch_rows(): return lax.psum_scatter(picked, 'y', scatter_dimension=0, tiled=True)  29.5 us
    all_to_all x1, blocking collectives, body(): lax.all_to_all(outgoing.reshape(EXPERTS, CAP, WIDTH), 'expert', split_axi...  19.1 us
    all_to_all x1, waiting for transfers between devices, body(): lax.all_to_all(summed[0], 'expert', split_axis=0, concat_axis=0, tiled=True)  14.1 us
  transfers between devices with their start and end apart: 5, of which 5 were waited for; matrix products, arithmetic and copies ran while one was open for 1% of the time, Pallas kernels for 0%

profile of v1, /device:TPU:1, one launch (start us, length us, event | category | flops | bytes accessed | tf_op | source)
XLA Modules:
  0.0 378.1 jit_solution(705764679827622156)
XLA Ops:
  6.6 0.7 all-gather.3.cloned.1.call-update
  7.3 0.1 constant_dynamic-slice_fusion
  7.4 0.1 copy.16
  7.5 0.1 reshape.15
  7.6 0.5 compare_convert_fusion
  8.1 0.6 fusion.idx_ref
  8.7 34.6 %all-gather.3.cloned.1.call-done.blocks_ref = bf16[8,128,1024]{2,1,0:T(8,128)(2,1)} async-done(((bf16[2,128,1024]{2,1,0:T(8,128)(2,1)}), bf16[8,128,1024]{2,1,0:T(8,128)(2,1)}) %all-gather.3.cloned.1.call-update) | async-done | bytes 2097168 | tf_op jit(solution)/shard_map/all_gather | solution.py:198
  43.3 6.0 %pick_blocks.1 = bf16[8,128,1024]{2,1,0:T(8,128)(2,1)} custom-call(s32[8]{0:T(128)} %fusion.idx_ref, s32[8]{0:T(128)} %get-tuple-element.9.mine_ref, bf16[8,128,1024]{2,1,0:T(8,128)(2,1)} %all-gather.3.cloned.1.call-done.blocks_ref), custom_call_target="tpu_custom_call" | custom-call | tf_op jit(solution)/shard_map/pick_blocks/pallas_call | solution.py:39
  49.4 0.0 all-gather.5.cloned.1.call-start
  49.4 0.6 dynamic_slice.6.len_ref
  50.0 29.5 %reduce-scatter.5.cloned.1.call-done = bf16[2,128,1024]{2,1,0:T(8,128)(2,1)} async-done(((bf16[8,128,1024]{2,1,0:T(8,128)(2,1)}), bf16[2,128,1024]{2,1,0:T(8,128)(2,1)}) %reduce-scatter.5.cloned.1.call-update) | async-done | bytes 524304 | tf_op jit(solution)/shard_map/reduce_scatter | solution.py:204
  79.5 1.0 copy-done.1
  80.6 4.2 %attend.1 = (bf16[256,768]{1,0:T(8,128)(2,1)S(1)}, bf16[640,768]{1,0:T(8,128)(2,1)S(1)}) custom-call(s32[1]{0:T(128)} %dynamic_slice.6.len_ref, bf16[256,1024]{1,0:T(8,128)(2,1)S(1)} %bitcast.9, s32[2,256]{1,0:T(2,128)S(1)} %bitcast.11), custom_call_target="tpu_custom_call" | custom-call | tf_op jit(solution)/shard_map/attend/pallas_call | solution.py:89
  84.8 19.1 %all_to_all.10.x_ref = bf16[8,80,768]{2,1,0:T(8,128)(2,1)S(1)} all-to-all(bf16[8,80,768]{2,1,0:T(8,128)(2,1)S(1)} %bitcast.8), channel_id=1, replica_groups=mesh['z'=4,'y'=4,'expert'=8] {'expert'}, dimensions={0} | all-to-all | bytes 1966080 | tf_op jit(solution)/shard_map/all_to_all | solution.py:222
  103.9 1.5 normalise.1
  105.4 0.0 reduce-scatter.7.cloned.1.call-start
  105.5 104.3 %all-gather.5.cloned.1.call-done.x_ref = bf16[1280,6144]{1,0:T(8,128)(2,1)} async-done(((bf16[80,6144]{1,0:T(8,128)(2,1)}), bf16[1280,6144]{1,0:T(8,128)(2,1)}) %all-gather.5.cloned.1.call-update) | async-done | bytes 15728656 | tf_op jit(solution)/shard_map/all_gather | solution.py:226
  209.8 34.9 %ffn.1 = bf16[16,8,80,768]{3,2,1,0:T(8,128)(2,1)} custom-call(bf16[1280,6144]{1,0:T(8,128)(2,1)} %all-gather.5.cloned.1.call-done.x_ref, bf16[1,6144,512]{2,1,0:T(8,128)(2,1)} %gate_ref.1, bf16[1,6144,512]{2,1,0:T(8,128)(2,1)} %up_ref.1, bf16[1,512,6144]{2,1,0:T(8,128)(2,1)} %down_ref.1), custom_call_target="tpu_custom_call" | custom-call | tf_op jit(solution)/shard_map/ffn/pallas_call | solution.py:145
  244.7 105.2 %reduce-scatter.7.cloned.1.call-done = bf16[1,8,80,768]{3,2,1,0:T(8,128)(2,1)} async-done(((bf16[16,8,80,768]{3,2,1,0:T(8,128)(2,1)}), bf16[1,8,80,768]{3,2,1,0:T(8,128)(2,1)}) %reduce-scatter.7.cloned.1.call-update) | async-done | bytes 983056
  349.8 5.3 %all-to-all-start.1 = ((bf16[8,80,768]{2,1,0:T(8,128)(2,1)}), bf16[8,80,768]{2,1,0:T(8,128)(2,1)S(1)}, u32[]{:S(2)}, u32[]{:S(2)}) async-start(bf16[8,80,768]{2,1,0:T(8,128)(2,1)} %bitcast.12), calls=%async_computation.2 | async-start | bytes 1966080 | tf_op jit(solution)/shard_map/all_to_all | solution.py:229
  355.1 0.1 copy.17.ids_ref
  355.3 0.1 copy.18.logits_ref
  355.4 14.1 %all-to-all-done.1 = bf16[8,80,768]{2,1,0:T(8,128)(2,1)S(1)} async-done(((bf16[8,80,768]{2,1,0:T(8,128)(2,1)}), bf16[8,80,768]{2,1,0:T(8,128)(2,1)S(1)}, u32[]{:S(2)}, u32[]{:S(2)}) %all-to-all-start.1) | async-done | bytes 983072 | tf_op jit(solution)/shard_map/all_to_all | solution.py:229
  369.5 2.0 combine.1
  (16 shorter events, 0.1 us)
Async XLA Ops:
  6.5 0.8 copy-start
  6.5 42.9 %copy-start.5 = (s32[16]{0:T(128)S(1)}, s32[16]{0:T(128)}, u32[]{:S(2)}) copy-start(s32[16]{0:T(128)} %param.11) | copy-start | bytes 196
  6.5 73.0 %copy-start.3 = (s32[256,2]{0,1:T(2,128)S(1)}, s32[256,2]{0,1:T(2,128)}, u32[]{:S(2)}) copy-start(s32[256,2]{0,1:T(2,128)} %param.14) | copy-start | bytes 6148
  6.5 97.4 %copy-start.2 = (f32[6144]{0:T(1024)S(1)}, f32[6144]{0:T(1024)}, u32[]{:S(2)}) copy-start(f32[6144]{0:T(1024)} %param.12) | copy-start | bytes 73732
  6.5 36.8 %all-gather.3.cloned.1.call-start = ((), (), s32[]{:S(2)}) async-start(), calls=%async_computation.4 | async-start | bytes 2621440 | tf_op jit(solution)/shard_map/all_gather | solution.py:198
  7.3 72.3 %reduce-scatter.5.cloned.1.call-start = ((), (), s32[]{:S(2)}) async-start(), calls=%async_computation.5 | async-start | bytes 2621440 | tf_op jit(solution)/shard_map/reduce_scatter | solution.py:204
  49.4 160.4 %all-gather.5.cloned.1.call-start = ((), (), s32[]{:S(2)}) async-start(), calls=%async_computation.6 | async-start | bytes 16711680 | tf_op jit(solution)/shard_map/all_gather | solution.py:226
  79.5 1.0 copy-start.1
  105.4 244.4 %reduce-scatter.7.cloned.1.call-start = ((), (), s32[]{:S(2)}) async-start(), calls=%async_computation.7 | async-start | bytes 16711680
  244.7 110.6 %copy-start.4 = (f32[256,2]{0,1:T(2,128)S(1)}, f32[256,2]{0,1:T(2,128)}, u32[]{:S(2)}) copy-start(f32[256,2]{0,1:T(2,128)} %param.13) | copy-start | bytes 6148
  349.8 19.7 %all-to-all-start.1 = ((bf16[8,80,768]{2,1,0:T(8,128)(2,1)}), bf16[8,80,768]{2,1,0:T(8,128)(2,1)S(1)}, u32[]{:S(2)}, u32[]{:S(2)}) async-start(bf16[8,80,768]{2,1,0:T(8,128)(2,1)} %bitcast.12), calls=%async_computation.2 | async-start | bytes 1966080 | tf_op jit(solution)/shard_map/all_to_all | solution.py:229
Sparse Core Ops, SparseCore 0:
  9.0 34.2 all-gather.2
  49.5 29.9 reduce-scatter.4
  105.5 104.1 all-gather.4
  244.8 104.9 reduce-scatter.6

commit v2 on v1

--- a/solution.py
+++ b/solution.py
@@ -125,37 +125,134 @@
     )(arrived, gain)
 
 
-def ffn_kernel(x_ref, gate_ref, up_ref, down_ref, out_ref):
-    x = x_ref[...]
-    gate = jnp.dot(x, gate_ref[0], preferred_element_type=jnp.float32)
-    up = jnp.dot(x, up_ref[0], preferred_element_type=jnp.float32)
-    hidden = (gate / (1.0 + jnp.exp(-gate)) * up).astype(jnp.bfloat16)
-    n = x.shape[0] // CAP
-    for i in range(EXPERTS):
-        part = jnp.dot(
-            hidden, down_ref[0, :, i * WIDTH : (i + 1) * WIDTH], preferred_element_type=jnp.float32
-        ).astype(jnp.bfloat16)
-        for j in range(n):
-            out_ref[j, i] = part[j * CAP : (j + 1) * CAP]
-
-
-def ffn(slot_rows, gate, up, down, tile):
-    n = slot_rows.shape[0]
-    whole = lambda i: (0, 0, 0)
+K_PARTS = 4
+K_PART = D // K_PARTS
+HALF = EXPERTS // 2
+
+
+def ffn_kernel(
+    x0, x1, x2, x3, gate_hbm, up_hbm, down_hbm, o0, o1, o2, o3,
+    xs, gate, up, down, outs, x_sem, gate_sem, up_sem, down_sem, out_sem,
+):
+    x_copies = [
+        pltpu.make_async_copy(x, xs.at[pl.ds(j * CAP, CAP)], x_sem.at[j])
+        for j, x in enumerate((x0, x1, x2, x3))
+    ]
+    in_copies = []
+    for k in range(K_PARTS):
+        rows = pl.ds(k * K_PART, K_PART)
+        in_copies.append(
+            (
+                pltpu.make_async_copy(gate_hbm.at[0, rows], gate.at[rows], gate_sem.at[k]),
+                pltpu.make_async_copy(up_hbm.at[0, rows], up.at[rows], up_sem.at[k]),
+            )
+        )
+    down_copies = [
+        pltpu.make_async_copy(
+            down_hbm.at[0, :, pl.ds(h * HALF * WIDTH, HALF * WIDTH)],
+            down.at[:, pl.ds(h * HALF * WIDTH, HALF * WIDTH)],
+            down_sem.at[h],
+        )
+        for h in range(2)
+    ]
+    for copy in x_copies:
+        copy.start()
+    for pair in in_copies:
+        for copy in pair:
+            copy.start()
+    for copy in down_copies:
+        copy.start()
+    for copy in x_copies:
+        copy.wait()
+    gate_part = up_part = None
+    for k, pair in enumerate(in_copies):
+        for copy in pair:
+            copy.wait()
+        rows = slice(k * K_PART, (k + 1) * K_PART)
+        x = xs[:, rows]
+        g = jnp.dot(x, gate[rows, :], preferred_element_type=jnp.float32)
+        u = jnp.dot(x, up[rows, :], preferred_element_type=jnp.float32)
+        gate_part = g if gate_part is None else gate_part + g
+        up_part = u if up_part is None else up_part + u
+    hidden = (gate_part / (1.0 + jnp.exp(-gate_part)) * up_part).astype(jnp.bfloat16)
+    out_copies = []
+    for h in range(2):
+        down_copies[h].wait()
+        for i in range(h * HALF, (h + 1) * HALF):
+            part = jnp.dot(
+                hidden, down[:, i * WIDTH : (i + 1) * WIDTH], preferred_element_type=jnp.float32
+            ).astype(jnp.bfloat16)
+            for j in range(SIDE):
+                outs[j, i] = part[j * CAP : (j + 1) * CAP]
+        for j, o in enumerate((o0, o1, o2, o3)):
+            some = pl.ds(h * HALF, HALF)
+            copy = pltpu.make_async_copy(outs.at[j, some], o.at[some], out_sem.at[h, j])
+            copy.start()
+            out_copies.append(copy)
+    for copy in out_copies:
+        copy.wait()
+
+
+def ffn(shards, gate, up, down):
+    anywhere = pl.BlockSpec(memory_space=pl.ANY)
     return pl.pallas_call(
         ffn_kernel,
-        grid=(n // tile,),
-        in_specs=[
-            pl.BlockSpec((tile, D), lambda i: (i, 0)),
-            pl.BlockSpec((1, D, FF_DEV), whole, pipeline_mode=pl.Buffered(1)),
-            pl.BlockSpec((1, D, FF_DEV), whole, pipeline_mode=pl.Buffered(1)),
-            pl.BlockSpec((1, FF_DEV, D), whole, pipeline_mode=pl.Buffered(1)),
+        in_specs=[anywhere] * 7,
+        out_specs=[anywhere] * SIDE,
+        out_shape=[jax.ShapeDtypeStruct((EXPERTS, CAP, WIDTH), jnp.bfloat16)] * SIDE,
+        scratch_shapes=[
+            pltpu.VMEM((SIDE * CAP, D), jnp.bfloat16),
+            pltpu.VMEM((D, FF_DEV), jnp.bfloat16),
+            pltpu.VMEM((D, FF_DEV), jnp.bfloat16),
+            pltpu.VMEM((FF_DEV, D), jnp.bfloat16),
+            pltpu.VMEM((SIDE, EXPERTS, CAP, WIDTH), jnp.bfloat16),
+            pltpu.SemaphoreType.DMA((SIDE,)),
+            pltpu.SemaphoreType.DMA((K_PARTS,)),
+            pltpu.SemaphoreType.DMA((K_PARTS,)),
+            pltpu.SemaphoreType.DMA((2,)),
+            pltpu.SemaphoreType.DMA((2, SIDE)),
         ],
-        out_specs=pl.BlockSpec((tile // CAP, EXPERTS, CAP, WIDTH), lambda i: (i, 0, 0, 0)),
-        out_shape=jax.ShapeDtypeStruct((n // CAP, EXPERTS, CAP, WIDTH), jnp.bfloat16),
-        compiler_params=pltpu.CompilerParams(vmem_limit_bytes=56 << 20),
+        compiler_params=pltpu.CompilerParams(vmem_limit_bytes=48 << 20),
+        cost_estimate=pl.CostEstimate(
+            flops=6 * SIDE * CAP * D * FF_DEV,
+            transcendentals=SIDE * CAP * FF_DEV,
+            bytes_accessed=6 * D * FF_DEV + 4 * SIDE * CAP * D,
+        ),
         name="ffn",
-    )(slot_rows, gate, up, down)
+    )(*shards, gate, up, down)
+
+
+def shift(value, first, step):
+    pairs = []
+    for z in range(SIDE):
+        for y in range(SIDE):
+            for e in range(EXPERTS):
+                along_y = (e % 2 == 0) == first
+                to_z, to_y = (z, (y + step) % SIDE) if along_y else ((z + step) % SIDE, y)
+                pairs.append(((z * SIDE + y) * EXPERTS + e, (to_z * SIDE + to_y) * EXPERTS + e))
+    return lax.ppermute(value, ("z", "y", "expert"), pairs)
+
+
+def add(*parts):
+    total = parts[0].astype(jnp.float32)
+    for part in parts[1:]:
+        total = total + part.astype(jnp.float32)
+    return total.astype(jnp.bfloat16)
+
+
+def experts(own, gate, up, down):
+    low, high = shift(own, True, 1), shift(own, True, -1)
+    firsts = {0: own, -1: low, 1: high, 2: shift(low, True, 1)}
+    sums = {}
+    for a, way in ((0, 1), (-1, -1), (1, 1), (2, -1)):
+        near = {step: shift(firsts[a], False, step) for step in (1, -1)}
+        far = shift(near[way], False, way)
+        here, to_low, to_high, to_far = ffn((firsts[a], near[1], near[-1], far), gate, up, down)
+        ahead, behind = (to_high, to_low) if way == 1 else (to_low, to_high)
+        passed = shift(to_far, False, way)
+        sums[a] = add(here, shift(add(ahead, passed), False, way), shift(behind, False, -way))
+    passed = shift(sums[2], True, 1)
+    return add(sums[0], shift(add(sums[1], passed), True, 1), shift(sums[-1], True, -1))
 
 
 def combine_kernel(att_ref, ret_ref, ids_ref, logits_ref, out_ref):
@@ -223,10 +320,8 @@
         outgoing.reshape(EXPERTS, CAP, WIDTH), "expert", split_axis=0, concat_axis=0, tiled=True
     )
     normed = normalise(arrived, norm_gain.reshape(1, D))
-    slot_rows = lax.all_gather(normed, ("z", "y"), axis=0, tiled=True)
-    partial = ffn(slot_rows, gate_weight, up_weight, down_weight, 320)
-    summed = lax.psum_scatter(partial, ("z", "y"), scatter_dimension=0, tiled=True)
-    returned = lax.all_to_all(summed[0], "expert", split_axis=0, concat_axis=0, tiled=True)
+    summed = experts(normed, gate_weight, up_weight, down_weight)
+    returned = lax.all_to_all(summed, "expert", split_axis=0, concat_axis=0, tiled=True)
     return combine(att, returned.reshape(EXPERTS * CAP, WIDTH), expert_ids, gate_logits)
 
 

time: 379 us -> 353 us (0.931); the launches traced: 378 us -> 347 us
  waiting for transfers between devices: 288 us -> 182 us
  starting transfers between devices: 5.45 us -> 43 us
  Pallas kernels: 48.6 us -> 75 us
  other arithmetic: 1.13 us -> 8.65 us
    unnamed x5 -> x2, waiting for transfers between devices: 106 us -> 0.73 us
    all_gather x1 -> x0, waiting for transfers between devices: 104 us -> none  [body(): slot_rows = lax.all_gather(normed, ('z', 'y'), axis=0, tiled=True)]
    ppermute x0 -> x30, waiting for transfers between devices: none -> 104 us  [shift(): return lax.ppermute(value, ('z', 'y', 'expert'), pairs)]
    ppermute x0 -> x30, starting transfers between devices: none -> 35.7 us  [shift(): return lax.ppermute(value, ('z', 'y', 'expert'), pairs)]
    pallas_call x1 -> x4, Pallas kernels: 34.9 us -> 61.9 us  [ffn(): pl.pallas_call(ffn_kernel, in_specs=[anywhere] * 7, out_specs=[anywhere]...]
    convert_element_type x0 -> x8, other arithmetic: none -> 7.63 us  [add(): return total.astype(jnp.bfloat16)]
  transfers between devices with their start and end apart: 5 -> 33, of which waited for: 5 -> 13; matrix products, arithmetic and copies ran while one was open for 1% -> 2% of each run, Pallas kernels for 0% -> 18%
where the time goes in v2:
time: 353 us; the launch traced here: 347 us
  waiting for transfers between devices  182 us (52%)
  Pallas kernels  75 us (21%)
  starting transfers between devices  43 us (12%)
  blocking collectives  19.1 us (5%)
  between operations  14.1 us (4%)
  other arithmetic  8.65 us (2%)
  local copies, waits for them, and re-layouts  4.8 us (1%)
    ppermute x30, waiting for transfers between devices, shift(): return lax.ppermute(value, ('z', 'y', 'expert'), pairs)  104 us
    pallas_call x4, Pallas kernels, ffn(): pl.pallas_call(ffn_kernel, in_specs=[anywhere] * 7, out_specs=[anywhere]...  61.9 us
    ppermute x30, starting transfers between devices, shift(): return lax.ppermute(value, ('z', 'y', 'expert'), pairs)  35.7 us
    all_gather x1, waiting for transfers between devices, fetch_rows(): column = lax.all_gather(records, 'z', axis=0, tiled=True)  34.7 us
    reduce_scatter x1, waiting for transfers between devices, fetch_rows(): return lax.psum_scatter(picked, 'y', scatter_dimension=0, tiled=True)  28.5 us
    all_to_all x1, blocking collectives, body(): lax.all_to_all(outgoing.reshape(EXPERTS, CAP, WIDTH), 'expert', split_axi...  19.1 us
    all_to_all x1, waiting for transfers between devices, body(): lax.all_to_all(summed, 'expert', split_axis=0, concat_axis=0, tiled=True)  14.1 us
    convert_element_type x8, other arithmetic, add(): return total.astype(jnp.bfloat16)  7.63 us
  transfers between devices with their start and end apart: 33, of which 13 were waited for; matrix products, arithmetic and copies ran while one was open for 2% of the time, Pallas kernels for 18%

profile of v2, /device:TPU:1, one launch (start us, length us, event | category | flops | bytes accessed | tf_op | source)
XLA Modules:
  0.0 347.0 jit_solution(923962734350629879)
XLA Ops:
  8.6 34.7 %all-gather.2.cloned.1.call-done.blocks_ref = bf16[8,128,1024]{2,1,0:T(8,128)(2,1)} async-done(((bf16[2,128,1024]{2,1,0:T(8,128)(2,1)}), bf16[8,128,1024]{2,1,0:T(8,128)(2,1)}) %all-gather.2.cloned.1.call-update) | async-done | bytes 2097168 | tf_op jit(solution)/shard_map/all_gather | solution.py:295
  43.3 6.3 %pick_blocks.1 = bf16[8,128,1024]{2,1,0:T(8,128)(2,1)} custom-call(s32[8]{0:T(128)} %fusion.idx_ref, s32[8]{0:T(128)} %get-tuple-element.41.mine_ref, bf16[8,128,1024]{2,1,0:T(8,128)(2,1)} %all-gather.2.cloned.1.call-done.blocks_ref), custom_call_target="tpu_custom_call" | custom-call | tf_op jit(solution)/shard_map/pick_blocks/pallas_call | solution.py:39
  50.9 28.5 %reduce-scatter.2.cloned.1.call-done = bf16[2,128,1024]{2,1,0:T(8,128)(2,1)} async-done(((bf16[8,128,1024]{2,1,0:T(8,128)(2,1)}), bf16[2,128,1024]{2,1,0:T(8,128)(2,1)}) %reduce-scatter.2.cloned.1.call-update) | async-done | bytes 524304 | tf_op jit(solution)/shard_map/reduce_scatter | solution.py:301
  80.5 4.2 %attend.1 = (bf16[256,768]{1,0:T(8,128)(2,1)S(1)}, bf16[640,768]{1,0:T(8,128)(2,1)S(1)}) custom-call(s32[1]{0:T(128)} %dynamic_slice.6.len_ref, bf16[256,1024]{1,0:T(8,128)(2,1)S(1)} %bitcast.7, s32[2,256]{1,0:T(2,128)S(1)} %bitcast.9), custom_call_target="tpu_custom_call" | custom-call | tf_op jit(solution)/shard_map/attend/pallas_call | solution.py:89
  84.7 19.1 %all_to_all.10.x_ref = bf16[8,80,768]{2,1,0:T(8,128)(2,1)S(1)} all-to-all(bf16[8,80,768]{2,1,0:T(8,128)(2,1)S(1)} %bitcast.6), channel_id=1, replica_groups=mesh['z'=4,'y'=4,'expert'=8] {'expert'}, dimensions={0} | all-to-all | bytes 1966080 | tf_op jit(solution)/shard_map/all_to_all | solution.py:319
  105.7 13.2 %collective-permute-done.13.x0 = bf16[80,6144]{1,0:T(8,128)(2,1)S(1)} collective-permute-done((bf16[80,6144]{1,0:T(8,128)(2,1)S(1)}, bf16[80,6144]{1,0:T(8,128)(2,1)S(1)}, u32[]{:S(2)}, u32[]{:S(2)}) %collective-permute-start.13) | collective-permute-done | bytes 983072 | tf_op jit(solution)/shard_map/ppermute | solution.py:233
  121.6 11.8 %collective-permute-done.14.x0 = bf16[80,6144]{1,0:T(8,128)(2,1)S(1)} collective-permute-done((bf16[80,6144]{1,0:T(8,128)(2,1)S(1)}, bf16[80,6144]{1,0:T(8,128)(2,1)S(1)}, u32[]{:S(2)}, u32[]{:S(2)}) %collective-permute-start.14) | collective-permute-done | bytes 983072 | tf_op jit(solution)/shard_map/ppermute | solution.py:233
  136.3 10.3 %collective-permute-done.16.x2 = bf16[80,6144]{1,0:T(8,128)(2,1)S(1)} collective-permute-done((bf16[80,6144]{1,0:T(8,128)(2,1)S(1)}, bf16[80,6144]{1,0:T(8,128)(2,1)S(1)}, u32[]{:S(2)}, u32[]{:S(2)}) %collective-permute-start.16) | collective-permute-done | bytes 983072 | tf_op jit(solution)/shard_map/ppermute | solution.py:233
  149.1 8.0 %collective-permute-done.24.x2 = bf16[80,6144]{1,0:T(8,128)(2,1)S(1)} collective-permute-done((bf16[80,6144]{1,0:T(8,128)(2,1)S(1)}, bf16[80,6144]{1,0:T(8,128)(2,1)S(1)}, u32[]{:S(2)}, u32[]{:S(2)}) %collective-permute-start.24) | collective-permute-done | bytes 983072 | tf_op jit(solution)/shard_map/ppermute | solution.py:233
  161.1 6.6 %collective-permute-done.17.x3 = bf16[80,6144]{1,0:T(8,128)(2,1)S(1)} collective-permute-done((bf16[80,6144]{1,0:T(8,128)(2,1)S(1)}, bf16[80,6144]{1,0:T(8,128)(2,1)S(1)}, u32[]{:S(2)}, u32[]{:S(2)}) %collective-permute-start.17) | collective-permute-done | bytes 983072 | tf_op jit(solution)/shard_map/ppermute | solution.py:233
  168.8 15.3 %ffn.6 = (bf16[8,80,768]{2,1,0:T(8,128)(2,1)S(1)}, bf16[8,80,768]{2,1,0:T(8,128)(2,1)S(1)}, bf16[8,80,768]{2,1,0:T(8,128)(2,1)}, bf16[8,80,768]{2,1,0:T(8,128)(2,1)S(1)}) custom-call(bf16[80,6144]{1,0:T(8,128)(2,1)S(1)} %collective-permute-done.14.x0, bf16[80,6144]{1,0:T(8,128)(2,1)S(1)} %collective-permute-done.15.x1, bf16[80,6144]{1,0:T(8,128)(2,1)} %copy-done.6, ...), custom_call_target="tpu_custom_call" | custom-call | flops 6039797760 | bytes 26738688 | tf_op jit(solution)/shard_map/ffn/pallas_call | solution.py:198
  184.1 2.7 collective-permute-start.1
  190.6 15.6 %ffn.7 = (bf16[8,80,768]{2,1,0:T(8,128)(2,1)S(1)}, bf16[8,80,768]{2,1,0:T(8,128)(2,1)S(1)}, bf16[8,80,768]{2,1,0:T(8,128)(2,1)S(1)}, bf16[8,80,768]{2,1,0:T(8,128)(2,1)}) custom-call(bf16[80,6144]{1,0:T(8,128)(2,1)S(1)} %collective-permute-done.13.x0, bf16[80,6144]{1,0:T(8,128)(2,1)S(1)} %collective-permute-done.23.x1, bf16[80,6144]{1,0:T(8,128)(2,1)} %copy-done.5, ...), custom_call_target="tpu_custom_call" | custom-call | flops 6039797760 | bytes 26738688 | tf_op jit(solution)/shard_map/ffn/pallas_call | solution.py:198
  206.5 15.6 %ffn.5 = (bf16[8,80,768]{2,1,0:T(8,128)(2,1)S(1)}, bf16[8,80,768]{2,1,0:T(8,128)(2,1)S(1)}, bf16[8,80,768]{2,1,0:T(8,128)(2,1)S(1)}, bf16[8,80,768]{2,1,0:T(8,128)(2,1)}) custom-call(bf16[80,6144]{1,0:T(8,128)(2,1)S(1)} %collective-permute-done.6.x0, bf16[80,6144]{1,0:T(8,128)(2,1)S(1)} %collective-permute-done.7.x1, ...), custom_call_target="tpu_custom_call" | custom-call | flops 6039797760 | bytes 26738688 | tf_op jit(solution)/shard_map/ffn/pallas_call | solution.py:198
  227.8 15.4 %ffn.4 = (bf16[8,80,768]{2,1,0:T(8,128)(2,1)S(1)}, bf16[8,80,768]{2,1,0:T(8,128)(2,1)S(1)}, bf16[8,80,768]{2,1,0:T(8,128)(2,1)S(1)}, bf16[8,80,768]{2,1,0:T(8,128)(2,1)S(1)}) custom-call(bf16[80,6144]{1,0:T(8,128)(2,1)S(1)} %normalise.1.x0, bf16[80,6144]{1,0:T(8,128)(2,1)S(1)} %collective-permute-done.x1, bf16[80,6144]{1,0:T(8,128)(2,1)} %collective-permute-done.1.x2, ...), custom_call_target="tpu_custom_call" | custom-call | flops 6039797760 | bytes 26738688 | tf_op jit(solution)/shard_map/ffn/pallas_call | solution.py:198
  245.1 2.7 collective-permute-start.27
  251.5 6.5 %collective-permute-done.3 = bf16[8,80,768]{2,1,0:T(8,128)(2,1)S(1)} collective-permute-done((bf16[8,80,768]{2,1,0:T(8,128)(2,1)S(1)}, bf16[8,80,768]{2,1,0:T(8,128)(2,1)S(1)}, u32[]{:S(2)}, u32[]{:S(2)}) %collective-permute-start.3) | collective-permute-done | bytes 983072 | tf_op jit(solution)/shard_map/ppermute | solution.py:233
  258.9 9.6 %collective-permute-done.28 = bf16[8,80,768]{2,1,0:T(8,128)(2,1)S(1)} collective-permute-done((bf16[8,80,768]{2,1,0:T(8,128)(2,1)S(1)}, bf16[8,80,768]{2,1,0:T(8,128)(2,1)S(1)}, u32[]{:S(2)}, u32[]{:S(2)}) %collective-permute-start.28) | collective-permute-done | bytes 983072 | tf_op jit(solution)/shard_map/ppermute | solution.py:233
  270.3 2.8 collective-permute-start.29
  273.1 12.1 %collective-permute-done.11 = bf16[8,80,768]{2,1,0:T(8,128)(2,1)S(1)} collective-permute-done((bf16[8,80,768]{2,1,0:T(8,128)(2,1)S(1)}, bf16[8,80,768]{2,1,0:T(8,128)(2,1)S(1)}, u32[]{:S(2)}, u32[]{:S(2)}) %collective-permute-start.11) | collective-permute-done | bytes 983072 | tf_op jit(solution)/shard_map/ppermute | solution.py:233
  288.2 11.9 %collective-permute-done.4 = bf16[8,80,768]{2,1,0:T(8,128)(2,1)S(1)} collective-permute-done((bf16[8,80,768]{2,1,0:T(8,128)(2,1)S(1)}, bf16[8,80,768]{2,1,0:T(8,128)(2,1)S(1)}, u32[]{:S(2)}, u32[]{:S(2)}) %collective-permute-start.4) | collective-permute-done | bytes 983072 | tf_op jit(solution)/shard_map/ppermute | solution.py:233
  300.1 14.2 %collective-permute-done.22 = bf16[8,80,768]{2,1,0:T(8,128)(2,1)S(1)} collective-permute-done((bf16[8,80,768]{2,1,0:T(8,128)(2,1)S(1)}, bf16[8,80,768]{2,1,0:T(8,128)(2,1)S(1)}, u32[]{:S(2)}, u32[]{:S(2)}) %collective-permute-start.22) | collective-permute-done | bytes 983072 | tf_op jit(solution)/shard_map/ppermute | solution.py:233
  315.9 7.3 %all-to-all-start.1 = ((bf16[8,80,768]{2,1,0:T(8,128)(2,1)}), bf16[8,80,768]{2,1,0:T(8,128)(2,1)S(1)}, u32[]{:S(2)}, u32[]{:S(2)}) async-start(bf16[8,80,768]{2,1,0:T(8,128)(2,1)} %add_convert_fusion), calls=%async_computation.2 | async-start | bytes 1966080 | tf_op jit(solution)/shard_map/all_to_all | solution.py:324
  323.5 14.1 %all-to-all-done.1 = bf16[8,80,768]{2,1,0:T(8,128)(2,1)S(1)} async-done(((bf16[8,80,768]{2,1,0:T(8,128)(2,1)}), bf16[8,80,768]{2,1,0:T(8,128)(2,1)S(1)}, u32[]{:S(2)}, u32[]{:S(2)}) %all-to-all-start.1) | async-done | bytes 983072 | tf_op jit(solution)/shard_map/all_to_all | solution.py:324
  (91 shorter events, 44.2 us)
Async XLA Ops:
  6.5 36.8 %all-gather.2.cloned.1.call-start = ((), (), s32[]{:S(2)}) async-start(), calls=%async_computation.3 | async-start | bytes 2621440 | tf_op jit(solution)/shard_map/all_gather | solution.py:295
  7.3 72.2 %reduce-scatter.2.cloned.1.call-start = ((), (), s32[]{:S(2)}) async-start(), calls=%async_computation.4 | async-start | bytes 2621440 | tf_op jit(solution)/shard_map/reduce_scatter | solution.py:301
  133.6 23.5 %collective-permute-start.24 = (bf16[80,6144]{1,0:T(8,128)(2,1)S(1)}, bf16[80,6144]{1,0:T(8,128)(2,1)S(1)}, u32[]{:S(2)}, u32[]{:S(2)}) collective-permute-start(bf16[80,6144]{1,0:T(8,128)(2,1)S(1)} %collective-permute-done.13.x0), channel_id=1, source_target_pairs={{0,96},{1,25},{2,98},{3,27},{4,100},{5,29},{6,102},{7,31},{8,104},... | collective-permute-start | bytes 2949128 | tf_op jit(solution)/shard_map/ppermute | solution.py:233
  134.2 22.9 %collective-permute-start.7 = (bf16[80,6144]{1,0:T(8,128)(2,1)S(1)}, bf16[80,6144]{1,0:T(8,128)(2,1)S(1)}, u32[]{:S(2)}, u32[]{:S(2)}) collective-permute-start(bf16[80,6144]{1,0:T(8,128)(2,1)S(1)} %collective-permute-done.6.x0), channel_id=1, source_target_pairs={{0,32},{1,9},{2,34},{3,11},{4,36},{5,13},{6,38},{7,15},{8,40},{9,1... | collective-permute-start | bytes 2949128 | tf_op jit(solution)/shard_map/ppermute | solution.py:233
  135.1 24.7 %collective-permute-start.15 = (bf16[80,6144]{1,0:T(8,128)(2,1)S(1)}, bf16[80,6144]{1,0:T(8,128)(2,1)S(1)}, u32[]{:S(2)}, u32[]{:S(2)}) collective-permute-start(bf16[80,6144]{1,0:T(8,128)(2,1)S(1)} %collective-permute-done.14.x0), channel_id=1, source_target_pairs={{0,32},{1,9},{2,34},{3,11},{4,36},{5,13},{6,38},{7,15},{8,40},{9,1... | collective-permute-start | bytes 2949128 | tf_op jit(solution)/shard_map/ppermute | solution.py:233
  149.1 35.1 %collective-permute-start = (bf16[80,6144]{1,0:T(8,128)(2,1)S(1)}, bf16[80,6144]{1,0:T(8,128)(2,1)S(1)}, u32[]{:S(2)}, u32[]{:S(2)}) collective-permute-start(bf16[80,6144]{1,0:T(8,128)(2,1)S(1)} %normalise.1.x0), channel_id=1, source_target_pairs={{0,32},{1,9},{2,34},{3,11},{4,36},{5,13},{6,38},{7,15},{8,40},{9,1... | collective-permute-start | bytes 2949128 | tf_op jit(solution)/shard_map/ppermute | solution.py:233
  157.1 29.8 %collective-permute-start.23 = (bf16[80,6144]{1,0:T(8,128)(2,1)S(1)}, bf16[80,6144]{1,0:T(8,128)(2,1)S(1)}, u32[]{:S(2)}, u32[]{:S(2)}) collective-permute-start(bf16[80,6144]{1,0:T(8,128)(2,1)S(1)} %collective-permute-done.13.x0), channel_id=1, source_target_pairs={{0,32},{1,9},{2,34},{3,11},{4,36},{5,13},{6,38},{7,15},{8,40},{9,1... | collective-permute-start | bytes 2949128 | tf_op jit(solution)/shard_map/ppermute | solution.py:233
  157.1 29.8 %collective-permute-start.25 = (bf16[80,6144]{1,0:T(8,128)(2,1)S(1)}, bf16[80,6144]{1,0:T(8,128)(2,1)S(1)}, u32[]{:S(2)}, u32[]{:S(2)}) collective-permute-start(bf16[80,6144]{1,0:T(8,128)(2,1)S(1)} %collective-permute-done.24.x2), channel_id=1, source_target_pairs={{0,96},{1,25},{2,98},{3,27},{4,100},{5,29},{6,102},{7,31},{8,104},... | collective-permute-start | bytes 2949128 | tf_op jit(solution)/shard_map/ppermute | solution.py:233
  159.8 46.3 %collective-permute-start.8 = (bf16[80,6144]{1,0:T(8,128)(2,1)S(1)}, bf16[80,6144]{1,0:T(8,128)(2,1)}, u32[]{:S(2)}, u32[]{:S(2)}) collective-permute-start(bf16[80,6144]{1,0:T(8,128)(2,1)S(1)} %collective-permute-done.6.x0), channel_id=1, source_target_pairs={{0,96},{1,25},{2,98},{3,27},{4,100},{5,29},{6,102},{7,31},{8,104},... | collective-permute-start | bytes 2949128 | tf_op jit(solution)/shard_map/ppermute | solution.py:233
  168.6 37.9 %collective-permute-start.9 = (bf16[80,6144]{1,0:T(8,128)(2,1)S(1)}, bf16[80,6144]{1,0:T(8,128)(2,1)}, u32[]{:S(2)}, u32[]{:S(2)}) collective-permute-start(bf16[80,6144]{1,0:T(8,128)(2,1)S(1)} %collective-permute-done.7.x1), channel_id=1, source_target_pairs={{0,32},{1,9},{2,34},{3,11},{4,36},{5,13},{6,38},{7,15},{8,40},{9,1... | collective-permute-start | bytes 2949128 | tf_op jit(solution)/shard_map/ppermute | solution.py:233
  184.1 41.0 %collective-permute-start.1 = (bf16[80,6144]{1,0:T(8,128)(2,1)S(1)}, bf16[80,6144]{1,0:T(8,128)(2,1)}, u32[]{:S(2)}, u32[]{:S(2)}) collective-permute-start(bf16[80,6144]{1,0:T(8,128)(2,1)S(1)} %normalise.1.x0), channel_id=1, source_target_pairs={{0,96},{1,25},{2,98},{3,27},{4,100},{5,29},{6,102},{7,31},{8,104},... | collective-permute-start | bytes 2949128 | tf_op jit(solution)/shard_map/ppermute | solution.py:233
  186.9 40.9 %collective-permute-start.2 = (bf16[80,6144]{1,0:T(8,128)(2,1)S(1)}, bf16[80,6144]{1,0:T(8,128)(2,1)}, u32[]{:S(2)}, u32[]{:S(2)}) collective-permute-start(bf16[80,6144]{1,0:T(8,128)(2,1)S(1)} %collective-permute-done.x1), channel_id=1, source_target_pairs={{0,32},{1,9},{2,34},{3,11},{4,36},{5,13},{6,38},{7,15},{8,40},{9,1... | collective-permute-start | bytes 2949128 | tf_op jit(solution)/shard_map/ppermute | solution.py:233
  187.9 35.7 %collective-permute-start.18 = (bf16[8,80,768]{2,1,0:T(8,128)(2,1)S(1)}, bf16[8,80,768]{2,1,0:T(8,128)(2,1)}, u32[]{:S(2)}, u32[]{:S(2)}) collective-permute-start(bf16[8,80,768]{2,1,0:T(8,128)(2,1)S(1)} %get-tuple-element.35), channel_id=1, source_target_pairs={{0,96},{1,25},{2,98},{3,27},{4,100},{5,29},{6,102},{7,31},{8,104},... | collective-permute-start | bytes 2949128 | tf_op jit(solution)/shard_map/ppermute | solution.py:233
  206.1 37.2 %collective-permute-start.26 = (bf16[8,80,768]{2,1,0:T(8,128)(2,1)}, bf16[8,80,768]{2,1,0:T(8,128)(2,1)}, u32[]{:S(2)}, u32[]{:S(2)}) collective-permute-start(bf16[8,80,768]{2,1,0:T(8,128)(2,1)} %get-tuple-element.39), channel_id=1, source_target_pairs={{0,96},{1,25},{2,98},{3,27},{4,100},{5,29},{6,102},{7,31},{8,104},... | collective-permute-start | bytes 2949128 | tf_op jit(solution)/shard_map/ppermute | solution.py:233
  222.1 23.0 %collective-permute-start.10 = (bf16[8,80,768]{2,1,0:T(8,128)(2,1)}, bf16[8,80,768]{2,1,0:T(8,128)(2,1)S(1)}, u32[]{:S(2)}, u32[]{:S(2)}) collective-permute-start(bf16[8,80,768]{2,1,0:T(8,128)(2,1)} %get-tuple-element.31), channel_id=1, source_target_pairs={{0,32},{1,9},{2,34},{3,11},{4,36},{5,13},{6,38},{7,15},{8,40},{9,1... | collective-permute-start | bytes 2949128 | tf_op jit(solution)/shard_map/ppermute | solution.py:233
  223.6 24.5 %collective-permute-start.20 = (bf16[8,80,768]{2,1,0:T(8,128)(2,1)}, bf16[8,80,768]{2,1,0:T(8,128)(2,1)}, u32[]{:S(2)}, u32[]{:S(2)}) collective-permute-start(bf16[8,80,768]{2,1,0:T(8,128)(2,1)} %get-tuple-element.36), channel_id=1, source_target_pairs={{0,32},{1,9},{2,34},{3,11},{4,36},{5,13},{6,38},{7,15},{8,40},{9,1... | collective-permute-start | bytes 2949128 | tf_op jit(solution)/shard_map/ppermute | solution.py:233
  225.1 24.4 %collective-permute-start.19 = (bf16[8,80,768]{2,1,0:T(8,128)(2,1)S(1)}, bf16[8,80,768]{2,1,0:T(8,128)(2,1)}, u32[]{:S(2)}, u32[]{:S(2)}) collective-permute-start(bf16[8,80,768]{2,1,0:T(8,128)(2,1)S(1)} %add_convert_fusion.5), channel_id=1, source_target_pairs={{0,96},{1,25},{2,98},{3,27},{4,100},{5,29},{6,102},{7,31},{8,104},... | collective-permute-start | bytes 2949128 | tf_op jit(solution)/shard_map/ppermute | solution.py:233
  243.3 25.1 %collective-permute-start.28 = (bf16[8,80,768]{2,1,0:T(8,128)(2,1)S(1)}, bf16[8,80,768]{2,1,0:T(8,128)(2,1)S(1)}, u32[]{:S(2)}, u32[]{:S(2)}) collective-permute-start(bf16[8,80,768]{2,1,0:T(8,128)(2,1)S(1)} %get-tuple-element.40), channel_id=1, source_target_pairs={{0,32},{1,9},{2,34},{3,11},{4,36},{5,13},{6,38},{7,15},{8,40},{9,1... | collective-permute-start | bytes 2949128 | tf_op jit(solution)/shard_map/ppermute | solution.py:233
  245.1 23.4 %collective-permute-start.27 = (bf16[8,80,768]{2,1,0:T(8,128)(2,1)S(1)}, bf16[8,80,768]{2,1,0:T(8,128)(2,1)S(1)}, u32[]{:S(2)}, u32[]{:S(2)}) collective-permute-start(bf16[8,80,768]{2,1,0:T(8,128)(2,1)S(1)} %add_convert_fusion.2), channel_id=1, source_target_pairs={{0,96},{1,25},{2,98},{3,27},{4,100},{5,29},{6,102},{7,31},{8,104},... | collective-permute-start | bytes 2949128 | tf_op jit(solution)/shard_map/ppermute | solution.py:233
  249.5 35.7 %collective-permute-start.11 = (bf16[8,80,768]{2,1,0:T(8,128)(2,1)S(1)}, bf16[8,80,768]{2,1,0:T(8,128)(2,1)S(1)}, u32[]{:S(2)}, u32[]{:S(2)}) collective-permute-start(bf16[8,80,768]{2,1,0:T(8,128)(2,1)S(1)} %add_convert_fusion.7), channel_id=1, source_target_pairs={{0,32},{1,9},{2,34},{3,11},{4,36},{5,13},{6,38},{7,15},{8,40},{9,1... | collective-permute-start | bytes 2949128 | tf_op jit(solution)/shard_map/ppermute | solution.py:233
  257.9 27.3 %collective-permute-start.21 = (bf16[8,80,768]{2,1,0:T(8,128)(2,1)S(1)}, bf16[8,80,768]{2,1,0:T(8,128)(2,1)S(1)}, u32[]{:S(2)}, u32[]{:S(2)}) collective-permute-start(bf16[8,80,768]{2,1,0:T(8,128)(2,1)S(1)} %add_convert_fusion.4), channel_id=1, source_target_pairs={{0,8},{1,33},{2,10},{3,35},{4,12},{5,37},{6,14},{7,39},{8,16},{9,4... | collective-permute-start | bytes 2949128 | tf_op jit(solution)/shard_map/ppermute | solution.py:233
  268.5 31.6 %collective-permute-start.4 = (bf16[8,80,768]{2,1,0:T(8,128)(2,1)S(1)}, bf16[8,80,768]{2,1,0:T(8,128)(2,1)S(1)}, u32[]{:S(2)}, u32[]{:S(2)}) collective-permute-start(bf16[8,80,768]{2,1,0:T(8,128)(2,1)S(1)} %add_convert_fusion.9), channel_id=1, source_target_pairs={{0,32},{1,9},{2,34},{3,11},{4,36},{5,13},{6,38},{7,15},{8,40},{9,1... | collective-permute-start | bytes 2949128 | tf_op jit(solution)/shard_map/ppermute | solution.py:233
  270.3 29.8 %collective-permute-start.29 = (bf16[8,80,768]{2,1,0:T(8,128)(2,1)S(1)}, bf16[8,80,768]{2,1,0:T(8,128)(2,1)S(1)}, u32[]{:S(2)}, u32[]{:S(2)}) collective-permute-start(bf16[8,80,768]{2,1,0:T(8,128)(2,1)S(1)} %add_convert_fusion.1), channel_id=1, source_target_pairs={{0,24},{1,97},{2,26},{3,99},{4,28},{5,101},{6,30},{7,103},{8,0},{9... | collective-permute-start | bytes 2949128 | tf_op jit(solution)/shard_map/ppermute | solution.py:233
  285.7 28.5 %collective-permute-start.22 = (bf16[8,80,768]{2,1,0:T(8,128)(2,1)S(1)}, bf16[8,80,768]{2,1,0:T(8,128)(2,1)S(1)}, u32[]{:S(2)}, u32[]{:S(2)}) collective-permute-start(bf16[8,80,768]{2,1,0:T(8,128)(2,1)S(1)} %add_convert_fusion.3), channel_id=1, source_target_pairs={{0,8},{1,33},{2,10},{3,35},{4,12},{5,37},{6,14},{7,39},{8,16},{9,4... | collective-permute-start | bytes 2949128 | tf_op jit(solution)/shard_map/ppermute | solution.py:233
  (20 other events, 327.5 us)
Sparse Core Ops, SparseCore 0:
  9.0 34.2 all-gather.1
  49.8 29.5 reduce-scatter.1

commit v3 on v2

--- a/solution.py
+++ b/solution.py
@@ -125,49 +125,58 @@
     )(arrived, gain)
 
 
-K_PARTS = 4
+K_PARTS = 6
 K_PART = D // K_PARTS
-HALF = EXPERTS // 2
+COL_PARTS = 4
+SIDES = EXPERTS // COL_PARTS
+HALF = FF_DEV // 2
+FF = 2 * FF_DEV
+SPANS = ((0, FF_DEV), (FF_DEV, HALF), (FF_DEV + HALF, HALF))
 
 
 def ffn_kernel(
-    x0, x1, x2, x3, gate_hbm, up_hbm, down_hbm, o0, o1, o2, o3,
-    xs, gate, up, down, outs, x_sem, gate_sem, up_sem, down_sem, out_sem,
+    x0, x1, x2, x3, g0, g1, g2, u0, u1, u2, d0, d1, d2, o0, o1, o2, o3,
+    xs, gate, up, down, outs, in_sem, out_sem,
 ):
-    x_copies = [
-        pltpu.make_async_copy(x, xs.at[pl.ds(j * CAP, CAP)], x_sem.at[j])
-        for j, x in enumerate((x0, x1, x2, x3))
-    ]
-    in_copies = []
+    stages = []
     for k in range(K_PARTS):
         rows = pl.ds(k * K_PART, K_PART)
-        in_copies.append(
-            (
-                pltpu.make_async_copy(gate_hbm.at[0, rows], gate.at[rows], gate_sem.at[k]),
-                pltpu.make_async_copy(up_hbm.at[0, rows], up.at[rows], up_sem.at[k]),
-            )
+        pairs = [
+            (x.at[:, rows], xs.at[pl.ds(j * CAP, CAP), rows])
+            for j, x in enumerate((x0, x1, x2, x3))
+        ]
+        for sources, target in (((g0, g1, g2), gate), ((u0, u1, u2), up)):
+            for source, (start, size) in zip(sources, SPANS):
+                pairs.append((source.at[rows], target.at[rows, pl.ds(start, size)]))
+        stages.append(pairs)
+    for h in range(COL_PARTS):
+        cols = pl.ds(h * SIDES * WIDTH, SIDES * WIDTH)
+        stages.append(
+            [
+                (source.at[:, cols], down.at[pl.ds(start, size), cols])
+                for source, (start, size) in zip((d0, d1, d2), SPANS)
+            ]
         )
-    down_copies = [
-        pltpu.make_async_copy(
-            down_hbm.at[0, :, pl.ds(h * HALF * WIDTH, HALF * WIDTH)],
-            down.at[:, pl.ds(h * HALF * WIDTH, HALF * WIDTH)],
-            down_sem.at[h],
-        )
-        for h in range(2)
+    stages = [
+        [pltpu.make_async_copy(a, b, in_sem.at[i, j]) for j, (a, b) in enumerate(pairs)]
+        for i, pairs in enumerate(stages)
     ]
-    for copy in x_copies:
-        copy.start()
-    for pair in in_copies:
-        for copy in pair:
-            copy.start()
-    for copy in down_copies:
-        copy.start()
-    for copy in x_copies:
-        copy.wait()
+
+    def begin(i):
+        if i < len(stages):
+            for copy in stages[i]:
+                copy.start()
+
+    def finish(i):
+        for copy in stages[i]:
+            copy.wait()
+        begin(i + 2)
+
+    begin(0)
+    begin(1)
     gate_part = up_part = None
-    for k, pair in enumerate(in_copies):
-        for copy in pair:
-            copy.wait()
+    for k in range(K_PARTS):
+        finish(k)
         rows = slice(k * K_PART, (k + 1) * K_PART)
         x = xs[:, rows]
         g = jnp.dot(x, gate[rows, :], preferred_element_type=jnp.float32)
@@ -176,16 +185,16 @@
         up_part = u if up_part is None else up_part + u
     hidden = (gate_part / (1.0 + jnp.exp(-gate_part)) * up_part).astype(jnp.bfloat16)
     out_copies = []
-    for h in range(2):
-        down_copies[h].wait()
-        for i in range(h * HALF, (h + 1) * HALF):
+    for h in range(COL_PARTS):
+        finish(K_PARTS + h)
+        for i in range(h * SIDES, (h + 1) * SIDES):
             part = jnp.dot(
                 hidden, down[:, i * WIDTH : (i + 1) * WIDTH], preferred_element_type=jnp.float32
             ).astype(jnp.bfloat16)
             for j in range(SIDE):
                 outs[j, i] = part[j * CAP : (j + 1) * CAP]
+        some = pl.ds(h * SIDES, SIDES)
         for j, o in enumerate((o0, o1, o2, o3)):
-            some = pl.ds(h * HALF, HALF)
             copy = pltpu.make_async_copy(outs.at[j, some], o.at[some], out_sem.at[h, j])
             copy.start()
             out_copies.append(copy)
@@ -197,40 +206,47 @@
     anywhere = pl.BlockSpec(memory_space=pl.ANY)
     return pl.pallas_call(
         ffn_kernel,
-        in_specs=[anywhere] * 7,
+        in_specs=[anywhere] * 13,
         out_specs=[anywhere] * SIDE,
         out_shape=[jax.ShapeDtypeStruct((EXPERTS, CAP, WIDTH), jnp.bfloat16)] * SIDE,
         scratch_shapes=[
             pltpu.VMEM((SIDE * CAP, D), jnp.bfloat16),
-            pltpu.VMEM((D, FF_DEV), jnp.bfloat16),
-            pltpu.VMEM((D, FF_DEV), jnp.bfloat16),
-            pltpu.VMEM((FF_DEV, D), jnp.bfloat16),
+            pltpu.VMEM((D, FF), jnp.bfloat16),
+            pltpu.VMEM((D, FF), jnp.bfloat16),
+            pltpu.VMEM((FF, D), jnp.bfloat16),
             pltpu.VMEM((SIDE, EXPERTS, CAP, WIDTH), jnp.bfloat16),
-            pltpu.SemaphoreType.DMA((SIDE,)),
-            pltpu.SemaphoreType.DMA((K_PARTS,)),
-            pltpu.SemaphoreType.DMA((K_PARTS,)),
-            pltpu.SemaphoreType.DMA((2,)),
-            pltpu.SemaphoreType.DMA((2, SIDE)),
+            pltpu.SemaphoreType.DMA((K_PARTS + COL_PARTS, 10)),
+            pltpu.SemaphoreType.DMA((COL_PARTS, SIDE)),
         ],
-        compiler_params=pltpu.CompilerParams(vmem_limit_bytes=48 << 20),
+        compiler_params=pltpu.CompilerParams(vmem_limit_bytes=58 << 20),
         cost_estimate=pl.CostEstimate(
-            flops=6 * SIDE * CAP * D * FF_DEV,
-            transcendentals=SIDE * CAP * FF_DEV,
-            bytes_accessed=6 * D * FF_DEV + 4 * SIDE * CAP * D,
+            flops=6 * SIDE * CAP * D * FF,
+            transcendentals=SIDE * CAP * FF,
+            bytes_accessed=6 * D * FF + 4 * SIDE * CAP * D,
         ),
         name="ffn",
-    )(*shards, gate, up, down)
-
-
-def shift(value, first, step):
+    )(*shards, *gate, *up, *down)
+
+
+def shift(value, doubled, step):
     pairs = []
     for z in range(SIDE):
         for y in range(SIDE):
             for e in range(EXPERTS):
-                along_y = (e % 2 == 0) == first
+                along_y = (e % 2 == 0) == doubled
                 to_z, to_y = (z, (y + step) % SIDE) if along_y else ((z + step) % SIDE, y)
                 pairs.append(((z * SIDE + y) * EXPERTS + e, (to_z * SIDE + to_y) * EXPERTS + e))
     return lax.ppermute(value, ("z", "y", "expert"), pairs)
+
+
+def trade(weight, dim):
+    low = lax.slice_in_dim(weight, 0, HALF, axis=dim)
+    high = lax.slice_in_dim(weight, HALF, FF_DEV, axis=dim)
+    return weight, shift(low, True, 1), shift(high, True, -1)
+
+
+def tie(*values):
+    return lax.optimization_barrier(values)
 
 
 def add(*parts):
@@ -241,18 +257,17 @@
 
 
 def experts(own, gate, up, down):
-    low, high = shift(own, True, 1), shift(own, True, -1)
-    firsts = {0: own, -1: low, 1: high, 2: shift(low, True, 1)}
-    sums = {}
-    for a, way in ((0, 1), (-1, -1), (1, 1), (2, -1)):
-        near = {step: shift(firsts[a], False, step) for step in (1, -1)}
-        far = shift(near[way], False, way)
-        here, to_low, to_high, to_far = ffn((firsts[a], near[1], near[-1], far), gate, up, down)
-        ahead, behind = (to_high, to_low) if way == 1 else (to_low, to_high)
-        passed = shift(to_far, False, way)
-        sums[a] = add(here, shift(add(ahead, passed), False, way), shift(behind, False, -way))
-    passed = shift(sums[2], True, 1)
-    return add(sums[0], shift(add(sums[1], passed), True, 1), shift(sums[-1], True, -1))
+    across, own_low, own_high = tie(shift(own, True, 2), shift(own, False, 1), shift(own, False, -1))
+    own_far, low, high = tie(shift(own_high, False, -1), shift(across, False, 1), shift(across, False, -1))
+    far = shift(high, False, -1)
+    sums = []
+    for shards in ((own, own_low, own_high, own_far), (across, low, high, far)):
+        here, to_low, to_high, to_far = ffn(shards, gate, up, down)
+        passed = shift(to_far, False, -1)
+        sums.append(
+            add(here, shift(to_high, False, 1), shift(add(to_low, passed), False, -1))
+        )
+    return add(sums[0], shift(sums[1], True, 2))
 
 
 def combine_kernel(att_ref, ret_ref, ids_ref, logits_ref, out_ref):
@@ -290,15 +305,17 @@
     )(att, returned, ids, logits)
 
 
-def fetch_rows(records, pair_blocks):
+def fetch_rows(records, pair_blocks, gate, up_weight):
     z, y = lax.axis_index("z"), lax.axis_index("y")
     column = lax.all_gather(records, "z", axis=0, tiled=True)
+    column, up_own, *gate = tie(column, up_weight, *gate)
     wanted = lax.dynamic_slice_in_dim(pair_blocks, z * SIDE, SIDE, 0).reshape(-1)
     owner = wanted // 2
     mine = (owner % SIDE == y).astype(jnp.int32)
     idx = (owner // SIDE) * 2 + wanted % 2
     picked = pick_blocks(idx, mine, column)
-    return lax.psum_scatter(picked, "y", scatter_dimension=0, tiled=True)
+    rows = lax.psum_scatter(picked, "y", scatter_dimension=0, tiled=True)
+    return rows, gate, up_own
 
 
 def body(
@@ -314,13 +331,18 @@
 ):
     dp_index = lax.axis_index("z") * SIDE + lax.axis_index("y")
     limit = lax.dynamic_slice_in_dim(lengths, dp_index, 1, 0)
-    rows = fetch_rows(records, pair_blocks).reshape(PROMPT, QKV)
+    gate = trade(gate_weight[0], 1)
+    rows, gate, up_own = fetch_rows(records, pair_blocks, gate, up_weight[0])
+    rows, down_own, *up = tie(rows, down_weight[0], *trade(up_own, 1))
+    rows = rows.reshape(PROMPT, QKV)
+    down = trade(down_own, 0)
     att, outgoing = attend(limit, rows, expert_ids.T)
     arrived = lax.all_to_all(
         outgoing.reshape(EXPERTS, CAP, WIDTH), "expert", split_axis=0, concat_axis=0, tiled=True
     )
+    arrived, *down = tie(arrived, *down)
     normed = normalise(arrived, norm_gain.reshape(1, D))
-    summed = experts(normed, gate_weight, up_weight, down_weight)
+    summed = experts(normed, gate, up, down)
     returned = lax.all_to_all(summed, "expert", split_axis=0, concat_axis=0, tiled=True)
     return combine(att, returned.reshape(EXPERTS * CAP, WIDTH), expert_ids, gate_logits)
 

time: 353 us -> 350 us (level); the launches traced: 347 us -> 350 us
  Pallas kernels: 75 us -> 52.7 us
  local copies, waits for them, and re-layouts: 4.8 us -> 17.4 us
  waiting for transfers between devices: 182 us -> 191 us
  blocking collectives: 19.1 us -> 26 us
  other arithmetic: 8.65 us -> 3.38 us
    ppermute x30 -> x20, waiting for transfers between devices: 104 us -> 177 us  [shift(): return lax.ppermute(value, ('z', 'y', 'expert'), pairs)]
    all_gather x1, waiting for transfers between devices: 34.7 us -> 0.01 us  [fetch_rows(): column = lax.all_gather(records, 'z', axis=0, tiled=True)]
    reduce_scatter x1, waiting for transfers between devices: 28.5 us -> 0.01 us  [fetch_rows(): rows = lax.psum_scatter(picked, 'y', scatter_dimension=0, tiled=True)]
    pallas_call x4 -> x2, Pallas kernels: 61.9 us -> 39.6 us  [ffn(): pl.pallas_call(ffn_kernel, in_specs=[anywhere] * 13, out_specs=[anywhere]...]
    slice x0 -> x3, local copies, waits for them, and re-layouts: none -> 14.5 us  [trade(): high = lax.slice_in_dim(weight, HALF, FF_DEV, axis=dim)]
    all_to_all x1, starting transfers between devices: 7.31 us -> 14.3 us  [body(): lax.all_to_all(summed, 'expert', split_axis=0, concat_axis=0, tiled=True)]
    all_to_all x1, blocking collectives: 19.1 us -> 26 us  [body(): lax.all_to_all(outgoing.reshape(EXPERTS, CAP, WIDTH), 'expert', split_axi...]
    convert_element_type x8 -> x4, other arithmetic: 7.63 us -> 2.36 us  [add(): return total.astype(jnp.bfloat16)]
  transfers between devices with their start and end apart: 33 -> 23, of which waited for: 13 -> 13; matrix products, arithmetic and copies ran while one was open for 2% -> 2% of each run, Pallas kernels for 18% -> 7%
where the time goes in v3:
time: 350 us
  waiting for transfers between devices  191 us (55%)
  Pallas kernels  52.7 us (15%)
  starting transfers between devices  45.8 us (13%)
  blocking collectives  26 us (7%)
  local copies, waits for them, and re-layouts  17.4 us (5%)
  between operations  13.6 us (4%)
    ppermute x20, waiting for transfers between devices, shift(): return lax.ppermute(value, ('z', 'y', 'expert'), pairs)  177 us
    pallas_call x2, Pallas kernels, ffn(): pl.pallas_call(ffn_kernel, in_specs=[anywhere] * 13, out_specs=[anywhere]...  39.6 us
    ppermute x20, starting transfers between devices, shift(): return lax.ppermute(value, ('z', 'y', 'expert'), pairs)  31.4 us
    all_to_all x1, blocking collectives, body(): lax.all_to_all(outgoing.reshape(EXPERTS, CAP, WIDTH), 'expert', split_axi...  26 us
    slice x3, local copies, waits for them, and re-layouts, trade(): high = lax.slice_in_dim(weight, HALF, FF_DEV, axis=dim)  14.5 us
    all_to_all x1, starting transfers between devices, body(): lax.all_to_all(summed, 'expert', split_axis=0, concat_axis=0, tiled=True)  14.3 us
    all_to_all x1, waiting for transfers between devices, body(): lax.all_to_all(summed, 'expert', split_axis=0, concat_axis=0, tiled=True)  14.1 us
  transfers between devices with their start and end apart: 23, of which 13 were waited for; matrix products, arithmetic and copies ran while one was open for 2% of the time, Pallas kernels for 7%

profile of v3, /device:TPU:1, one launch (start us, length us, event | category | flops | bytes accessed | tf_op | source)
XLA Modules:
  0.0 349.6 jit_solution(14196983225666828230)
XLA Ops:
  6.5 5.0 %fusion.3 = (bf16[6144,256]{1,0:T(8,128)(2,1)S(1)}, bf16[6144,256]{1,0:T(8,128)(2,1)}) fusion(bf16[6144,512]{1,0:T(8,128)(2,1)} %bitcast.13), kind=kLoop, calls=%fused_computation.20 | loop fusion | bytes 12582912 | tf_op jit(solution)/shard_map/slice | solution.py:244
  17.5 50.5 %collective-permute-done.g1 = bf16[6144,256]{1,0:T(8,128)(2,1)} collective-permute-done((bf16[6144,256]{1,0:T(8,128)(2,1)}, bf16[6144,256]{1,0:T(8,128)(2,1)}, u32[]{:S(2)}, u32[]{:S(2)}) %collective-permute-start) | collective-permute-done | bytes 3145760 | tf_op jit(solution)/shard_map/ppermute | solution.py:239
  67.9 6.3 %pick_blocks.1 = bf16[8,128,1024]{2,1,0:T(8,128)(2,1)} custom-call(s32[8]{0:T(128)} %fusion.idx_ref, s32[8]{0:T(128)} %get-tuple-element.65.mine_ref, bf16[8,128,1024]{2,1,0:T(8,128)(2,1)} %all-gather.2.cloned.1.call-done.blocks_ref), custom_call_target="tpu_custom_call" | custom-call | tf_op jit(solution)/shard_map/pick_blocks/pallas_call | solution.py:39
  74.3 3.3 fusion.2
  80.3 34.9 %collective-permute-done.2.u1 = bf16[6144,256]{1,0:T(8,128)(2,1)S(1)} collective-permute-done((bf16[6144,256]{1,0:T(8,128)(2,1)S(1)}, bf16[6144,256]{1,0:T(8,128)(2,1)S(1)}, u32[]{:S(2)}, u32[]{:S(2)}) %collective-permute-start.2) | collective-permute-done | bytes 3145760 | tf_op jit(solution)/shard_map/ppermute | solution.py:239
  117.0 6.3 %fusion.1 = (bf16[256,6144]{1,0:T(8,128)(2,1)}, bf16[256,6144]{1,0:T(8,128)(2,1)}) fusion(bf16[512,6144]{1,0:T(8,128)(2,1)} %bitcast.19), kind=kLoop, calls=%fused_computation.18 | loop fusion | bytes 12582912 | tf_op jit(solution)/shard_map/slice | solution.py:244
  126.6 4.2 %attend.1 = (bf16[256,768]{1,0:T(8,128)(2,1)S(1)}, bf16[640,768]{1,0:T(8,128)(2,1)S(1)}) custom-call(s32[1]{0:T(128)} %dynamic_slice.6.len_ref, bf16[256,1024]{1,0:T(8,128)(2,1)S(1)} %bitcast.10, s32[2,256]{1,0:T(2,128)S(1)} %bitcast.12), custom_call_target="tpu_custom_call" | custom-call | tf_op jit(solution)/shard_map/attend/pallas_call | solution.py:89
  130.8 26.0 %all_to_all.10.x_ref = bf16[8,80,768]{2,1,0:T(8,128)(2,1)S(1)} all-to-all(bf16[8,80,768]{2,1,0:T(8,128)(2,1)S(1)} %bitcast.9), channel_id=1, replica_groups=mesh['z'=4,'y'=4,'expert'=8] {'expert'}, dimensions={0} | all-to-all | bytes 1966080 | tf_op jit(solution)/shard_map/all_to_all | solution.py:340
  156.8 4.5 %collective-permute-done.4.d1 = bf16[256,6144]{1,0:T(8,128)(2,1)} collective-permute-done((bf16[256,6144]{1,0:T(8,128)(2,1)}, bf16[256,6144]{1,0:T(8,128)(2,1)}, u32[]{:S(2)}, u32[]{:S(2)}) %collective-permute-start.4) | collective-permute-done | bytes 3145760 | tf_op jit(solution)/shard_map/ppermute | solution.py:239
  165.9 12.3 %collective-permute-done.6.x0 = bf16[80,6144]{1,0:T(8,128)(2,1)S(1)} collective-permute-done((bf16[80,6144]{1,0:T(8,128)(2,1)S(1)}, bf16[80,6144]{1,0:T(8,128)(2,1)S(1)}, u32[]{:S(2)}, u32[]{:S(2)}) %collective-permute-start.6) | collective-permute-done | bytes 983072 | tf_op jit(solution)/shard_map/ppermute | solution.py:239
  178.2 11.2 %collective-permute-done.7.x1 = bf16[80,6144]{1,0:T(8,128)(2,1)S(1)} collective-permute-done((bf16[80,6144]{1,0:T(8,128)(2,1)S(1)}, bf16[80,6144]{1,0:T(8,128)(2,1)S(1)}, u32[]{:S(2)}, u32[]{:S(2)}) %collective-permute-start.7) | collective-permute-done | bytes 983072 | tf_op jit(solution)/shard_map/ppermute | solution.py:239
  193.7 10.3 %collective-permute-done.10.x1 = bf16[80,6144]{1,0:T(8,128)(2,1)S(1)} collective-permute-done((bf16[80,6144]{1,0:T(8,128)(2,1)S(1)}, bf16[80,6144]{1,0:T(8,128)(2,1)S(1)}, u32[]{:S(2)}, u32[]{:S(2)}) %collective-permute-start.10) | collective-permute-done | bytes 983072 | tf_op jit(solution)/shard_map/ppermute | solution.py:239
  204.0 9.8 %collective-permute-done.9.x3 = bf16[80,6144]{1,0:T(8,128)(2,1)S(1)} collective-permute-done((bf16[80,6144]{1,0:T(8,128)(2,1)S(1)}, bf16[80,6144]{1,0:T(8,128)(2,1)S(1)}, u32[]{:S(2)}, u32[]{:S(2)}) %collective-permute-start.9) | collective-permute-done | bytes 983072 | tf_op jit(solution)/shard_map/ppermute | solution.py:239
  213.8 3.1 collective-permute-start.15
  217.0 11.0 %collective-permute-done.15.x3 = bf16[80,6144]{1,0:T(8,128)(2,1)} collective-permute-done((bf16[80,6144]{1,0:T(8,128)(2,1)S(1)}, bf16[80,6144]{1,0:T(8,128)(2,1)}, u32[]{:S(2)}, u32[]{:S(2)}) %collective-permute-start.15) | collective-permute-done | bytes 983072 | tf_op jit(solution)/shard_map/ppermute | solution.py:239
  228.0 19.8 %ffn.3 = (bf16[8,80,768]{2,1,0:T(8,128)(2,1)}, bf16[8,80,768]{2,1,0:T(8,128)(2,1)}, bf16[8,80,768]{2,1,0:T(8,128)(2,1)}, bf16[8,80,768]{2,1,0:T(8,128)(2,1)}) custom-call(bf16[80,6144]{1,0:T(8,128)(2,1)} %copy-done.15, bf16[80,6144]{1,0:T(8,128)(2,1)} %copy-done.17, bf16[80,6144]{1,0:T(8,128)(2,1)} %copy-done.18, ...), custom_call_target="tpu_custom_call" | custom-call | flops 12079595520 | bytes 45613056 | tf_op jit(solution)/shard_map/ffn/pallas_call | solution.py:207
  247.9 3.5 %collective-permute-start.17 = (bf16[8,80,768]{2,1,0:T(8,128)(2,1)}, bf16[8,80,768]{2,1,0:T(8,128)(2,1)S(1)}, u32[]{:S(2)}, u32[]{:S(2)}) collective-permute-start(bf16[8,80,768]{2,1,0:T(8,128)(2,1)} %get-tuple-element.64), channel_id=1, source_target_pairs={{0,96},{1,25},{2,98},{3,27},{4,100},{5,29},{6,102},{7,31},{8,104},... | collective-permute-start | bytes 2949128 | tf_op jit(solution)/shard_map/ppermute | solution.py:239
  251.4 19.8 %ffn.2 = (bf16[8,80,768]{2,1,0:T(8,128)(2,1)}, bf16[8,80,768]{2,1,0:T(8,128)(2,1)}, bf16[8,80,768]{2,1,0:T(8,128)(2,1)}, bf16[8,80,768]{2,1,0:T(8,128)(2,1)}) custom-call(bf16[80,6144]{1,0:T(8,128)(2,1)} %copy-done.2, bf16[80,6144]{1,0:T(8,128)(2,1)} %copy-done.12, bf16[80,6144]{1,0:T(8,128)(2,1)} %copy-done.13, bf16[80,6144]{1,0:T(8,128)(2,1)} %copy-done.16, ...), custom_call_target="tpu_custom_call" | custom-call | flops 12079595520 | bytes 45613056 | tf_op jit(solution)/shard_map/ffn/pallas_call | solution.py:207
  274.6 10.2 %collective-permute-done.13 = bf16[8,80,768]{2,1,0:T(8,128)(2,1)S(1)} collective-permute-done((bf16[8,80,768]{2,1,0:T(8,128)(2,1)}, bf16[8,80,768]{2,1,0:T(8,128)(2,1)S(1)}, u32[]{:S(2)}, u32[]{:S(2)}) %collective-permute-start.13) | collective-permute-done | bytes 983072 | tf_op jit(solution)/shard_map/ppermute | solution.py:239
  286.7 8.6 %collective-permute-done.18 = bf16[8,80,768]{2,1,0:T(8,128)(2,1)S(1)} collective-permute-done((bf16[8,80,768]{2,1,0:T(8,128)(2,1)S(1)}, bf16[8,80,768]{2,1,0:T(8,128)(2,1)S(1)}, u32[]{:S(2)}, u32[]{:S(2)}) %collective-permute-start.18) | collective-permute-done | bytes 983072 | tf_op jit(solution)/shard_map/ppermute | solution.py:239
  297.3 10.1 %collective-permute-done.14 = bf16[8,80,768]{2,1,0:T(8,128)(2,1)S(1)} collective-permute-done((bf16[8,80,768]{2,1,0:T(8,128)(2,1)S(1)}, bf16[8,80,768]{2,1,0:T(8,128)(2,1)S(1)}, u32[]{:S(2)}, u32[]{:S(2)}) %collective-permute-start.14) | collective-permute-done | bytes 983072 | tf_op jit(solution)/shard_map/ppermute | solution.py:239
  307.4 3.1 collective-permute-done.19
  312.0 14.3 %all-to-all-start.1 = ((bf16[8,80,768]{2,1,0:T(8,128)(2,1)}), bf16[8,80,768]{2,1,0:T(8,128)(2,1)S(1)}, u32[]{:S(2)}, u32[]{:S(2)}) async-start(bf16[8,80,768]{2,1,0:T(8,128)(2,1)} %add_convert_fusion), calls=%async_computation.2 | async-start | bytes 1966080 | tf_op jit(solution)/shard_map/all_to_all | solution.py:346
  326.6 14.1 %all-to-all-done.1 = bf16[8,80,768]{2,1,0:T(8,128)(2,1)S(1)} async-done(((bf16[8,80,768]{2,1,0:T(8,128)(2,1)}), bf16[8,80,768]{2,1,0:T(8,128)(2,1)S(1)}, u32[]{:S(2)}, u32[]{:S(2)}) %all-to-all-start.1) | async-done | bytes 983072 | tf_op jit(solution)/shard_map/all_to_all | solution.py:346
  (86 shorter events, 33.8 us)
Async XLA Ops:
  6.5 61.4 %all-gather.2.cloned.1.call-start = ((), (), s32[]{:S(2)}) async-start(), calls=%async_computation.3 | async-start | bytes 2621440 | tf_op jit(solution)/shard_map/all_gather | solution.py:310
  11.5 56.4 %collective-permute-start = (bf16[6144,256]{1,0:T(8,128)(2,1)}, bf16[6144,256]{1,0:T(8,128)(2,1)}, u32[]{:S(2)}, u32[]{:S(2)}) collective-permute-start(bf16[6144,256]{1,0:T(8,128)(2,1)} %get-tuple-element.72), channel_id=1, source_target_pairs={{0,8},{1,33},{2,10},{3,35},{4,12},{5,37},{6,14},{7,39},{8,16},{9,4... | collective-permute-start | bytes 9437192 | tf_op jit(solution)/shard_map/ppermute | solution.py:239
  14.0 53.9 %collective-permute-start.1 = (bf16[6144,256]{1,0:T(8,128)(2,1)S(1)}, bf16[6144,256]{1,0:T(8,128)(2,1)}, u32[]{:S(2)}, u32[]{:S(2)}) collective-permute-start(bf16[6144,256]{1,0:T(8,128)(2,1)S(1)} %get-tuple-element.71), channel_id=1, source_target_pairs={{0,24},{1,97},{2,26},{3,99},{4,28},{5,101},{6,30},{7,103},{8,0},{9... | collective-permute-start | bytes 9437192 | tf_op jit(solution)/shard_map/ppermute | solution.py:239
  16.1 100.8 %reduce-scatter.2.cloned.1.call-start = ((), (), s32[]{:S(2)}) async-start(), calls=%async_computation.4 | async-start | bytes 2621440 | tf_op jit(solution)/shard_map/reduce_scatter | solution.py:317
  77.5 37.7 %collective-permute-start.2 = (bf16[6144,256]{1,0:T(8,128)(2,1)S(1)}, bf16[6144,256]{1,0:T(8,128)(2,1)S(1)}, u32[]{:S(2)}, u32[]{:S(2)}) collective-permute-start(bf16[6144,256]{1,0:T(8,128)(2,1)S(1)} %get-tuple-element.70), channel_id=1, source_target_pairs={{0,8},{1,33},{2,10},{3,35},{4,12},{5,37},{6,14},{7,39},{8,16},{9,4... | collective-permute-start | bytes 9437192 | tf_op jit(solution)/shard_map/ppermute | solution.py:239
  78.0 38.9 %collective-permute-start.3 = (bf16[6144,256]{1,0:T(8,128)(2,1)S(1)}, bf16[6144,256]{1,0:T(8,128)(2,1)}, u32[]{:S(2)}, u32[]{:S(2)}) collective-permute-start(bf16[6144,256]{1,0:T(8,128)(2,1)S(1)} %get-tuple-element.69), channel_id=1, source_target_pairs={{0,24},{1,97},{2,26},{3,99},{4,28},{5,101},{6,30},{7,103},{8,0},{9... | collective-permute-start | bytes 9437192 | tf_op jit(solution)/shard_map/ppermute | solution.py:239
  123.3 37.9 %collective-permute-start.4 = (bf16[256,6144]{1,0:T(8,128)(2,1)}, bf16[256,6144]{1,0:T(8,128)(2,1)}, u32[]{:S(2)}, u32[]{:S(2)}) collective-permute-start(bf16[256,6144]{1,0:T(8,128)(2,1)} %get-tuple-element.68), channel_id=1, source_target_pairs={{0,8},{1,33},{2,10},{3,35},{4,12},{5,37},{6,14},{7,39},{8,16},{9,4... | collective-permute-start | bytes 9437192 | tf_op jit(solution)/shard_map/ppermute | solution.py:239
  123.3 37.9 %collective-permute-start.5 = (bf16[256,6144]{1,0:T(8,128)(2,1)}, bf16[256,6144]{1,0:T(8,128)(2,1)}, u32[]{:S(2)}, u32[]{:S(2)}) collective-permute-start(bf16[256,6144]{1,0:T(8,128)(2,1)} %get-tuple-element.67), channel_id=1, source_target_pairs={{0,24},{1,97},{2,26},{3,99},{4,28},{5,101},{6,30},{7,103},{8,0},{9... | collective-permute-start | bytes 9437192 | tf_op jit(solution)/shard_map/ppermute | solution.py:239
  161.8 86.0 %copy-start.2 = (bf16[80,6144]{1,0:T(8,128)(2,1)}, bf16[80,6144]{1,0:T(8,128)(2,1)S(1)}, u32[]{:S(2)}) copy-start(bf16[80,6144]{1,0:T(8,128)(2,1)S(1)} %normalise.1.x0) | copy-start | bytes 2949124
  161.8 16.5 %collective-permute-start.6 = (bf16[80,6144]{1,0:T(8,128)(2,1)S(1)}, bf16[80,6144]{1,0:T(8,128)(2,1)S(1)}, u32[]{:S(2)}, u32[]{:S(2)}) collective-permute-start(bf16[80,6144]{1,0:T(8,128)(2,1)S(1)} %normalise.1.x0), channel_id=1, source_target_pairs={{0,16},{1,65},{2,18},{3,67},{4,20},{5,69},{6,22},{7,71},{8,24},{9,... | collective-permute-start | bytes 2949128 | tf_op jit(solution)/shard_map/ppermute | solution.py:239
  163.2 26.3 %collective-permute-start.7 = (bf16[80,6144]{1,0:T(8,128)(2,1)S(1)}, bf16[80,6144]{1,0:T(8,128)(2,1)S(1)}, u32[]{:S(2)}, u32[]{:S(2)}) collective-permute-start(bf16[80,6144]{1,0:T(8,128)(2,1)S(1)} %normalise.1.x0), channel_id=1, source_target_pairs={{0,32},{1,9},{2,34},{3,11},{4,36},{5,13},{6,38},{7,15},{8,40},{9,1... | collective-permute-start | bytes 2949128 | tf_op jit(solution)/shard_map/ppermute | solution.py:239
  164.5 25.0 %collective-permute-start.8 = (bf16[80,6144]{1,0:T(8,128)(2,1)S(1)}, bf16[80,6144]{1,0:T(8,128)(2,1)S(1)}, u32[]{:S(2)}, u32[]{:S(2)}) collective-permute-start(bf16[80,6144]{1,0:T(8,128)(2,1)S(1)} %normalise.1.x0), channel_id=1, source_target_pairs={{0,96},{1,25},{2,98},{3,27},{4,100},{5,29},{6,102},{7,31},{8,104},... | collective-permute-start | bytes 2949128 | tf_op jit(solution)/shard_map/ppermute | solution.py:239
  189.5 14.5 %collective-permute-start.10 = (bf16[80,6144]{1,0:T(8,128)(2,1)S(1)}, bf16[80,6144]{1,0:T(8,128)(2,1)S(1)}, u32[]{:S(2)}, u32[]{:S(2)}) collective-permute-start(bf16[80,6144]{1,0:T(8,128)(2,1)S(1)} %collective-permute-done.6.x0), channel_id=1, source_target_pairs={{0,32},{1,9},{2,34},{3,11},{4,36},{5,13},{6,38},{7,15},{8,40},{9,1... | collective-permute-start | bytes 2949128 | tf_op jit(solution)/shard_map/ppermute | solution.py:239
  189.6 14.5 %collective-permute-start.11 = (bf16[80,6144]{1,0:T(8,128)(2,1)S(1)}, bf16[80,6144]{1,0:T(8,128)(2,1)S(1)}, u32[]{:S(2)}, u32[]{:S(2)}) collective-permute-start(bf16[80,6144]{1,0:T(8,128)(2,1)S(1)} %collective-permute-done.6.x0), channel_id=1, source_target_pairs={{0,96},{1,25},{2,98},{3,27},{4,100},{5,29},{6,102},{7,31},{8,104},... | collective-permute-start | bytes 2949128 | tf_op jit(solution)/shard_map/ppermute | solution.py:239
  192.3 21.6 %collective-permute-start.9 = (bf16[80,6144]{1,0:T(8,128)(2,1)S(1)}, bf16[80,6144]{1,0:T(8,128)(2,1)S(1)}, u32[]{:S(2)}, u32[]{:S(2)}) collective-permute-start(bf16[80,6144]{1,0:T(8,128)(2,1)S(1)} %collective-permute-done.8.x2), channel_id=1, source_target_pairs={{0,96},{1,25},{2,98},{3,27},{4,100},{5,29},{6,102},{7,31},{8,104},... | collective-permute-start | bytes 2949128 | tf_op jit(solution)/shard_map/ppermute | solution.py:239
  213.8 14.2 %collective-permute-start.15 = (bf16[80,6144]{1,0:T(8,128)(2,1)S(1)}, bf16[80,6144]{1,0:T(8,128)(2,1)}, u32[]{:S(2)}, u32[]{:S(2)}) collective-permute-start(bf16[80,6144]{1,0:T(8,128)(2,1)S(1)} %collective-permute-done.11.x2), channel_id=1, source_target_pairs={{0,96},{1,25},{2,98},{3,27},{4,100},{5,29},{6,102},{7,31},{8,104},... | collective-permute-start | bytes 2949128 | tf_op jit(solution)/shard_map/ppermute | solution.py:239
  247.9 24.9 %collective-permute-start.17 = (bf16[8,80,768]{2,1,0:T(8,128)(2,1)}, bf16[8,80,768]{2,1,0:T(8,128)(2,1)S(1)}, u32[]{:S(2)}, u32[]{:S(2)}) collective-permute-start(bf16[8,80,768]{2,1,0:T(8,128)(2,1)} %get-tuple-element.64), channel_id=1, source_target_pairs={{0,96},{1,25},{2,98},{3,27},{4,100},{5,29},{6,102},{7,31},{8,104},... | collective-permute-start | bytes 2949128 | tf_op jit(solution)/shard_map/ppermute | solution.py:239
  271.2 13.5 %collective-permute-start.13 = (bf16[8,80,768]{2,1,0:T(8,128)(2,1)}, bf16[8,80,768]{2,1,0:T(8,128)(2,1)S(1)}, u32[]{:S(2)}, u32[]{:S(2)}) collective-permute-start(bf16[8,80,768]{2,1,0:T(8,128)(2,1)} %get-tuple-element.58), channel_id=1, source_target_pairs={{0,96},{1,25},{2,98},{3,27},{4,100},{5,29},{6,102},{7,31},{8,104},... | collective-permute-start | bytes 2949128 | tf_op jit(solution)/shard_map/ppermute | solution.py:239
  271.4 15.2 %collective-permute-start.16 = (bf16[8,80,768]{2,1,0:T(8,128)(2,1)S(1)}, bf16[8,80,768]{2,1,0:T(8,128)(2,1)S(1)}, u32[]{:S(2)}, u32[]{:S(2)}) collective-permute-start(bf16[8,80,768]{2,1,0:T(8,128)(2,1)S(1)} %copy-done.14), channel_id=1, source_target_pairs={{0,32},{1,9},{2,34},{3,11},{4,36},{5,13},{6,38},{7,15},{8,40},{9,1... | collective-permute-start | bytes 2949128 | tf_op jit(solution)/shard_map/ppermute | solution.py:239
  273.0 22.2 %collective-permute-start.18 = (bf16[8,80,768]{2,1,0:T(8,128)(2,1)S(1)}, bf16[8,80,768]{2,1,0:T(8,128)(2,1)S(1)}, u32[]{:S(2)}, u32[]{:S(2)}) collective-permute-start(bf16[8,80,768]{2,1,0:T(8,128)(2,1)S(1)} %add_convert_fusion.2), channel_id=1, source_target_pairs={{0,96},{1,25},{2,98},{3,27},{4,100},{5,29},{6,102},{7,31},{8,104},... | collective-permute-start | bytes 2949128 | tf_op jit(solution)/shard_map/ppermute | solution.py:239
  274.5 22.8 %collective-permute-start.12 = (bf16[8,80,768]{2,1,0:T(8,128)(2,1)}, bf16[8,80,768]{2,1,0:T(8,128)(2,1)S(1)}, u32[]{:S(2)}, u32[]{:S(2)}) collective-permute-start(bf16[8,80,768]{2,1,0:T(8,128)(2,1)} %get-tuple-element.56), channel_id=1, source_target_pairs={{0,32},{1,9},{2,34},{3,11},{4,36},{5,13},{6,38},{7,15},{8,40},{9,1... | collective-permute-start | bytes 2949128 | tf_op jit(solution)/shard_map/ppermute | solution.py:239
  285.0 22.4 %collective-permute-start.14 = (bf16[8,80,768]{2,1,0:T(8,128)(2,1)S(1)}, bf16[8,80,768]{2,1,0:T(8,128)(2,1)S(1)}, u32[]{:S(2)}, u32[]{:S(2)}) collective-permute-start(bf16[8,80,768]{2,1,0:T(8,128)(2,1)S(1)} %add_convert_fusion.4), channel_id=1, source_target_pairs={{0,96},{1,25},{2,98},{3,27},{4,100},{5,29},{6,102},{7,31},{8,104},... | collective-permute-start | bytes 2949128 | tf_op jit(solution)/shard_map/ppermute | solution.py:239
  295.6 14.9 %collective-permute-start.19 = (bf16[8,80,768]{2,1,0:T(8,128)(2,1)S(1)}, bf16[8,80,768]{2,1,0:T(8,128)(2,1)S(1)}, u32[]{:S(2)}, u32[]{:S(2)}) collective-permute-start(bf16[8,80,768]{2,1,0:T(8,128)(2,1)S(1)} %add_convert_fusion.1), channel_id=1, source_target_pairs={{0,16},{1,65},{2,18},{3,67},{4,20},{5,69},{6,22},{7,71},{8,24},{9,... | collective-permute-start | bytes 2949128 | tf_op jit(solution)/shard_map/ppermute | solution.py:239
  312.0 28.7 %all-to-all-start.1 = ((bf16[8,80,768]{2,1,0:T(8,128)(2,1)}), bf16[8,80,768]{2,1,0:T(8,128)(2,1)S(1)}, u32[]{:S(2)}, u32[]{:S(2)}) async-start(bf16[8,80,768]{2,1,0:T(8,128)(2,1)} %add_convert_fusion), calls=%async_computation.2 | async-start | bytes 1966080 | tf_op jit(solution)/shard_map/all_to_all | solution.py:346
  (19 other events, 467.0 us)
Sparse Core Ops, SparseCore 0:
  16.2 40.4 all-gather.1
  74.4 39.0 reduce-scatter.1
